TPU v7x, 256 devices: a whole 4x4x8 slice. The times are simulated.
256 devices in a mesh: view: 2 (over x_hi), seq: 8 (over y, core), event: 16 (over x_lo, z).
Axes of the slice: x: 4 (x_hi: 2, x_lo: 2; x = x_hi * 2 + x_lo), y: 4, z: 8, core: 2. Of those that a mesh axis runs over, the one named last changes fastest.
Arguments:
- query: bfloat16 [16, 2, 3072, 512], P('event', 'view', 'seq'), may hold values from -7 to 7
- key: bfloat16 [16, 2, 3072, 512], P('event', 'view', 'seq'), may hold values from -7 to 7
- value: bfloat16 [16, 2, 3072, 512], P('event', 'view', 'seq'), may hold values from -6 to 6
- pattern: int32 [16, 2, 24, 24], P('event', 'view', 'seq'), may hold values from 0 to 1, as said below
- out_weight: bfloat16 [512, 512], replicated, may hold values from -0.25 to 0.25
- served: int32 [16, 2, 128, 128], P('event', 'view', 'seq'), may hold values from 0 to 383
- anchor_rows: int32 [16, 2, 2048], P('event', 'view', 'seq'), may hold values from 0 to 383
- positive_slot: int32 [16, 2, 2048], P('event', 'view', 'seq'), may hold values from 0 to 2047, as said below
- anchor_live: int32 [16, 2, 2048], P('event', 'view', 'seq'), may hold values from 0 to 1, as said below
Outputs:
- mixed: bfloat16 [16, 2, 3072, 512], P('event', 'view', 'seq')
- grad_wo: float32 [512, 512], replicated
- loss: float32 [], replicated
Inputs may be any that keep to these rules, and one draw needn't show every extreme that they name: pattern[e, v, b, b] is 1 for every block b. `positive_slot`: for an anchor of view v the slot lies in [(1 - v) * 1024, (2 - v) * 1024), a point of the other view. `anchor_live`: every device's block of 256 anchors holds at least one live anchor.
All inputs are finite; a program needn't handle non-finite values.
Results may differ from a plain program's by a relative error of at most 0.015.
Values may be sent and summed in bfloat16 or wider, within the bound.
No kernel may reach another device: no remote copies, remote signals or barrier semaphores. Data moves between devices by JAX's collectives and lax.ppermute only.
A program may use at most 64 MiB of HBM per device.

v0:
```python
import jax
import jax.numpy as jnp
from jax import lax
from jax.sharding import PartitionSpec as P

HEADS = 16
BLOCK = 128


NEGATIVE = -1e30
SHARPNESS_SCALE = 0.07


def from_behind(array, axis, by):
    peers = lax.axis_size(axis)
    return lax.ppermute(array, axis, [(i, (i + by) % peers) for i in range(peers)])


def per_device(
    query, key, value, pattern, out_weight, served, anchor_rows, positive_slot, anchor_live
):
    queries = query[0, 0]
    keys = key[0, 0]
    values = value[0, 0]
    points, width = queries.shape
    head_dim = width // HEADS
    scale = head_dim ** (-0.5)
    loop_size = lax.axis_size("seq")
    myself = lax.axis_index("seq")
    local_pattern = pattern[0, 0].astype(jnp.float32)
    blocks_dev, blocks_all = local_pattern.shape
    query_block = jnp.arange(points) // BLOCK
    pick_rows = (query_block[:, None] == jnp.arange(blocks_dev)[None, :]).astype(jnp.float32)
    row_pattern = jnp.dot(pick_rows, local_pattern, preferred_element_type=jnp.float32)
    head_queries = queries.reshape(points, HEADS, head_dim)

    def attend(state, key_piece, value_piece, start):
        length = key_piece.shape[0]
        count = length // BLOCK
        size = BLOCK
        key_groups = key_piece.reshape(count, size, width)
        value_groups = value_piece.reshape(count, size, width)
        offsets = start + jnp.arange(count, dtype=jnp.int32) * size

        def one_group(carry, inputs):
            key_group, value_group, offset = inputs
            key_block = (offset + jnp.arange(size)) // BLOCK
            pick_keys = (jnp.arange(blocks_all)[:, None] == key_block[None, :]).astype(jnp.float32)
            allowed = jnp.dot(row_pattern, pick_keys, preferred_element_type=jnp.float32) > 0.5
            best, total, accum = carry
            head_keys = key_group.reshape(size, HEADS, head_dim)
            head_values = value_group.reshape(size, HEADS, head_dim)
            scores = (
                jnp.einsum(
                    "qhd,khd->hqk", head_queries, head_keys, preferred_element_type=jnp.float32
                )
                * scale
            )
            scores = jnp.where(allowed[None], scores, NEGATIVE)
            new_best = jnp.maximum(best, jnp.max(scores, axis=-1))
            weights = jnp.where(allowed[None], jnp.exp(scores - new_best[..., None]), 0.0)
            factor = jnp.exp(best - new_best)
            total = total * factor + jnp.sum(weights, axis=-1)
            added = jnp.einsum(
                "hqk,khd->hqd",
                weights.astype(jnp.bfloat16),
                head_values,
                preferred_element_type=jnp.float32,
            )
            result = (new_best, total, accum * factor[..., None] + added)
            return (result, None)

        final_state, unused = lax.scan(one_group, state, (key_groups, value_groups, offsets))
        return final_state

    initial = (
        jnp.full((HEADS, points), NEGATIVE, jnp.float32),
        jnp.zeros((HEADS, points), jnp.float32),
        jnp.zeros((HEADS, points, head_dim), jnp.float32),
    )
    state = attend(initial, keys, values, myself * points)
    moving = (keys, values)
    for step in range(1, loop_size):
        moving = from_behind((moving[0], moving[1]), "seq", 1)
        root = (myself - step) % loop_size
        state = attend(state, moving[0], moving[1], root * points)
    best, total, accum = state
    mixed = (
        (accum / total[..., None]).transpose(1, 0, 2).reshape(points, width).astype(jnp.bfloat16)
    )
    embedding_rows = jnp.dot(mixed, out_weight, preferred_element_type=jnp.float32)
    inverse = lax.rsqrt(jnp.sum(embedding_rows * embedding_rows, axis=-1) + 1e-06)
    unit = (embedding_rows * inverse[:, None]).astype(jnp.bfloat16)
    served_rows = served[0, 0]
    senders, capacity = served_rows.shape
    flat_served = served_rows.reshape(-1)
    outgoing = jnp.take(unit, flat_served, axis=0).reshape(senders, capacity, width)
    incoming = lax.all_to_all(outgoing, ("view", "seq"), split_axis=0, concat_axis=0, tiled=True)
    contender_vectors = incoming.reshape(senders * capacity, width)
    own_rows = anchor_rows[0, 0]
    query_vectors = jnp.take(unit, own_rows, axis=0)
    pairwise_scores = (
        lax.dot_general(
            query_vectors,
            contender_vectors,
            (((1,), (1,)), ((), ())),
            preferred_element_type=jnp.float32,
        )
        / SHARPNESS_SCALE
    )
    exponentiated_scores = jnp.exp(pairwise_scores)
    partition_totals = jnp.sum(exponentiated_scores, axis=-1)
    log_total = jnp.log(partition_totals)
    correct_column = (
        jnp.arange(senders * capacity)[None, :] == positive_slot[0, 0][:, None]
    ).astype(jnp.float32)
    active_queries = anchor_live[0, 0].astype(jnp.float32)
    loss_part = jnp.sum(
        active_queries * (log_total - jnp.sum(pairwise_scores * correct_column, axis=-1))
    )
    live_part = jnp.sum(active_queries)
    score_derivatives = (
        active_queries[:, None]
        * (exponentiated_scores / partition_totals[:, None] - correct_column)
        / SHARPNESS_SCALE
    )
    anchor_grads = jnp.dot(
        score_derivatives, contender_vectors.astype(jnp.float32), precision=lax.Precision.HIGHEST
    )
    candidate_grads = lax.dot_general(
        score_derivatives,
        query_vectors.astype(jnp.float32),
        (((0,), (0,)), ((), ())),
        precision=lax.Precision.HIGHEST,
    )
    returned = lax.all_to_all(
        candidate_grads.reshape(senders, capacity, width).astype(jnp.bfloat16),
        ("view", "seq"),
        split_axis=0,
        concat_axis=0,
        tiled=True,
    ).astype(jnp.float32)
    unit_grads = (
        jnp.zeros((points, width), jnp.float32).at[flat_served].add(returned.reshape(-1, width))
    )
    unit_grads = unit_grads.at[own_rows].add(anchor_grads)
    inner = jnp.sum(embedding_rows * unit_grads, axis=-1)
    embedding_gradients = (
        inverse[:, None] * (unit_grads - embedding_rows * (inverse * inverse * inner)[:, None])
    ).astype(jnp.bfloat16)
    loss_term = lax.dot_general(
        mixed, embedding_gradients, (((0,), (0,)), ((), ())), preferred_element_type=jnp.float32
    )
    grad_total, loss_total, live_total = lax.psum(
        (loss_term, loss_part, live_part), ("view", "seq", "event")
    )
    return (mixed[None, None], grad_total, loss_total / live_total)


def solution(mesh):
    placed = (
        P("event", "view", "seq", None),
        P("event", "view", "seq", None),
        P("event", "view", "seq", None),
        P("event", "view", "seq", None),
        P(),
        P("event", "view", "seq", None),
        P("event", "view", "seq"),
        P("event", "view", "seq"),
        P("event", "view", "seq"),
    )
    return jax.shard_map(
        per_device,
        mesh=mesh,
        in_specs=placed,
        out_specs=(P("event", "view", "seq", None), P(), P()),
        check_vma=False,
    )
```

profile of v0, /device:TPU:1, one launch (start us, length us, event | category | flops | bytes accessed | tf_op | source)
XLA Modules:
  0.0 610.0 jit_solution(11017529696734789384)
XLA Ops:
  12.2 31.8 %while.136 = (s32[]{:T(128)}, f32[16,384]{1,0:T(8,128)S(1)}, f32[16,384]{1,0:T(8,128)S(1)}, f32[16,384,32]{1,2,0:T(8,128)S(1)}, s32[3]{0:T(128)S(1)}, /*index=5*...) while((s32[]{:T(128)}, f32[16,384]{1,0:T(8,128)S(1)}, ...), condition=%wide.region_3.4_spmd.clone, body=%wide.region_0.3_spmd.clone.sunk | while | flops 113921024 | bytes 13323405 | solution.py:73
  19.9 2.8 fusion.319
  30.5 2.8 fusion.319
  41.1 2.8 fusion.319
  45.9 26.6 %while.129 = (s32[]{:T(128)}, f32[16,384]{1,0:T(8,128)S(1)}, f32[16,384]{1,0:T(8,128)S(1)}, f32[16,384,32]{1,2,0:T(8,128)S(1)}, s32[3]{0:T(128)S(1)}, /*index=5*...) while((s32[]{:T(128)}, f32[16,384]{1,0:T(8,128)S(1)}, ...), condition=%wide.region_7.8_spmd, body=%wide.region_4.7_spmd.sunk | while | flops 113705984 | bytes 25906324 | solution.py:73
  51.9 2.8 fusion.255
  69.7 2.8 fusion.255
  73.9 26.6 %while.130 = (s32[]{:T(128)}, f32[16,384]{1,0:T(8,128)S(1)}, f32[16,384]{1,0:T(8,128)S(1)}, f32[16,384,32]{1,2,0:T(8,128)S(1)}, s32[3]{0:T(128)S(1)}, /*index=5*...) while((s32[]{:T(128)}, f32[16,384]{1,0:T(8,128)S(1)}, ...), condition=%wide.region_11.12_spmd, body=%wide.region_8.11_spmd.sunk | while | flops 113705984 | bytes 25906324 | solution.py:73
  97.7 2.8 fusion.264
  102.6 26.6 %while.131 = (s32[]{:T(128)}, f32[16,384]{1,0:T(8,128)S(1)}, f32[16,384]{1,0:T(8,128)S(1)}, f32[16,384,32]{1,2,0:T(8,128)S(1)}, s32[3]{0:T(128)S(1)}, /*index=5*...) while((s32[]{:T(128)}, f32[16,384]{1,0:T(8,128)S(1)}, ...), condition=%wide.region_15.16_spmd, body=%wide.region_12.15_spmd.sunk | while | flops 113705984 | bytes 25906324 | solution.py:73
  129.8 26.6 %while.132 = (s32[]{:T(128)}, f32[16,384]{1,0:T(8,128)S(1)}, f32[16,384]{1,0:T(8,128)S(1)}, f32[16,384,32]{1,2,0:T(8,128)S(1)}, s32[3]{0:T(128)S(1)}, /*index=5*...) while((s32[]{:T(128)}, f32[16,384]{1,0:T(8,128)S(1)}, ...), condition=%wide.region_19.20_spmd, body=%wide.region_16.19_spmd.sunk | while | flops 113705984 | bytes 25906324 | solution.py:73
  157.6 26.6 %while.133 = (s32[]{:T(128)}, f32[16,384]{1,0:T(8,128)S(1)}, f32[16,384]{1,0:T(8,128)S(1)}, f32[16,384,32]{1,2,0:T(8,128)S(1)}, s32[3]{0:T(128)S(1)}, /*index=5*...) while((s32[]{:T(128)}, f32[16,384]{1,0:T(8,128)S(1)}, ...), condition=%wide.region_23.24_spmd, body=%wide.region_20.23_spmd.sunk | while | flops 113705984 | bytes 25906324 | solution.py:73
  185.6 26.0 %while.134 = (s32[]{:T(128)}, f32[16,384]{1,0:T(8,128)S(1)}, f32[16,384]{1,0:T(8,128)S(1)}, f32[16,384,32]{1,2,0:T(8,128)S(1)}, s32[3]{0:T(128)S(1)}, /*index=5*...) while((s32[]{:T(128)}, f32[16,384]{1,0:T(8,128)S(1)}, ...), condition=%wide.region_27.28_spmd, body=%wide.region_24.27_spmd.sunk | while | flops 113705984 | bytes 25906324 | solution.py:73
  211.6 23.4 %while.135 = (s32[]{:T(128)}, f32[16,384]{1,0:T(8,128)S(1)}, f32[16,384]{1,0:T(8,128)S(1)}, f32[16,384,32]{1,2,0:T(8,128)S(1)}, s32[3]{0:T(128)S(1)}, /*index=5*...) while((s32[]{:T(128)}, f32[16,384]{1,0:T(8,128)S(1)}, ...), condition=%wide.region_31.32_spmd, body=%wide.region_28.31_spmd.sunk | while | flops 113705984 | bytes 25906324 | solution.py:73
  235.7 9.2 %gather_fusion.1 = bf16[2048,512]{1,0:T(8,128)(2,1)} fusion(bf16[384,512]{1,0:T(8,128)(2,1)S(1)} %multiply_convert_fusion.1, s32[2048]{0:T(1024)S(1)} %broadcast_clamp_fusion), kind=kCustom, calls=%fused_computation.1 | custom fusion | bytes 4202496 | tf_op jit(solution)/shard_map/jit(_take)/gather | solution.py:97
  247.6 6.5 %all-to-all-start = ((bf16[16,128,512]{2,1,0:T(8,128)(2,1)}), bf16[16,128,512]{2,1,0:T(8,128)(2,1)}, u32[]{:S(2)}, u32[]{:S(2)}) async-start(bf16[16,128,512]{2,1,0:T(8,128)(2,1)} %broadcast_select_fusion), calls=%async_computation | async-start | bytes 4194304 | tf_op jit(solution)/shard_map/all_to_all | solution.py:98
  255.3 27.4 %all-to-all-done = bf16[16,128,512]{2,1,0:T(8,128)(2,1)} async-done(((bf16[16,128,512]{2,1,0:T(8,128)(2,1)}), bf16[16,128,512]{2,1,0:T(8,128)(2,1)}, u32[]{:S(2)}, u32[]{:S(2)}) %all-to-all-start) | async-done | bytes 2097184 | tf_op jit(solution)/shard_map/all_to_all | solution.py:98
  285.3 3.8 convolution_convert_fusion
  289.0 7.1 %all-to-all-start.1 = ((bf16[16,128,512]{2,1,0:T(8,128)(2,1)}), bf16[16,128,512]{2,1,0:T(8,128)(2,1)}, u32[]{:S(2)}, u32[]{:S(2)}) async-start(bf16[16,128,512]{2,1,0:T(8,128)(2,1)} %bitcast.422), calls=%async_computation.1 | async-start | bytes 4194304 | tf_op jit(solution)/shard_map/all_to_all | solution.py:136
  296.2 4.5 fusion.136
  300.7 24.1 %all-to-all-done.1 = bf16[16,128,512]{2,1,0:T(8,128)(2,1)} async-done(((bf16[16,128,512]{2,1,0:T(8,128)(2,1)}), bf16[16,128,512]{2,1,0:T(8,128)(2,1)}, u32[]{:S(2)}, u32[]{:S(2)}) %all-to-all-start.1) | async-done | bytes 2097184 | tf_op jit(solution)/shard_map/all_to_all | solution.py:136
  324.8 13.5 %scatter_custom_fusion = f32[384,512]{1,0:T(8,128)S(1)} fusion(s32[2048]{0:T(1024)} %bitcast.431, bf16[2048,512]{1,0:T(8,128)(2,1)} %bitcast.76, f32[]{:T(128)} %constant.623.clone.1), kind=kCustom, calls=%fused_computation.191 | custom fusion | flops 2097152 | bytes 2884096 | tf_op jit(solution)/shard_map/scatter-add | solution.py:144
  344.6 81.8 %all-reduce = (f32[]{:T(128)}, f32[]{:T(128)}) all-reduce(f32[]{:T(128)} %multiply_reduce_fusion.2, f32[]{:T(128)} %convert_reduce_fusion), channel_id=1, replica_groups=mesh['view'=2,'seq'=8,'event'=16] {'view','seq','event'}, use_global_device_ids=true, to_apply=%region_40.41 | all-reduce | flops 2 | bytes 16 | tf_op jit(solution)/shard_map/psum | solution.py:154
  427.8 172.0 %all-reduce.3.cloned.1.call-done = f32[512,512]{1,0:T(8,128)} async-done(((f32[512,512]{1,0:T(8,128)}), f32[512,512]{1,0:T(8,128)}) %all-reduce.3.cloned.1.call-update) | async-done | bytes 1048592 | tf_op jit(solution)/shard_map/psum | solution.py:154
  (405 shorter events, 224.4 us)
Async XLA Ops:
  7.2 227.9 %copy-start = (bf16[512,512]{1,0:T(8,128)(2,1)S(1)}, bf16[512,512]{1,0:T(8,128)(2,1)}, u32[]{:S(2)}) copy-start(bf16[512,512]{1,0:T(8,128)(2,1)} %param.29) | copy-start | bytes 1572868
  7.2 37.0 %collective-permute-start = (bf16[384,512]{1,0:T(8,128)(2,1)}, bf16[384,512]{1,0:T(8,128)(2,1)}, u32[]{:S(2)}, u32[]{:S(2)}) collective-permute-start(bf16[384,512]{1,0:T(8,128)(2,1)} %bitcast.423), channel_id=1, source_target_pairs={{0,16},{16,32},{32,48},{48,64},{64,80},{80,96},{96,112},{112,0},{1... | collective-permute-start | bytes 1179656 | tf_op jit(solution)/shard_map/ppermute | solution.py:16
  9.9 35.9 %collective-permute-start.1 = (bf16[384,512]{1,0:T(8,128)(2,1)}, bf16[384,512]{1,0:T(8,128)(2,1)}, u32[]{:S(2)}, u32[]{:S(2)}) collective-permute-start(bf16[384,512]{1,0:T(8,128)(2,1)} %bitcast.425), channel_id=1, source_target_pairs={{0,16},{16,32},{32,48},{48,64},{64,80},{80,96},{96,112},{112,0},{1... | collective-permute-start | bytes 1179656 | tf_op jit(solution)/shard_map/ppermute | solution.py:16
  12.2 31.9 %copy-start.8 = (s32[1,1,16,128]{3,2,1,0:T(8,128)S(1)}, s32[1,1,16,128]{3,2,1,0:T(8,128)}, u32[]{:S(2)}) copy-start(s32[1,1,16,128]{3,2,1,0:T(8,128)} %param.30) | copy-start | bytes 24580
  44.1 1.8 copy-start.9
  44.2 28.3 %collective-permute-start.2 = (bf16[384,512]{1,0:T(8,128)(2,1)}, bf16[384,512]{1,0:T(8,128)(2,1)}, u32[]{:S(2)}, u32[]{:S(2)}) collective-permute-start(bf16[384,512]{1,0:T(8,128)(2,1)} %collective-permute-done), channel_id=1, source_target_pairs={{0,16},{16,32},{32,48},{48,64},{64,80},{80,96},{96,112},{112,0},{1... | collective-permute-start | bytes 1179656 | tf_op jit(solution)/shard_map/ppermute | solution.py:16
  45.8 28.0 %collective-permute-start.3 = (bf16[384,512]{1,0:T(8,128)(2,1)}, bf16[384,512]{1,0:T(8,128)(2,1)}, u32[]{:S(2)}, u32[]{:S(2)}) collective-permute-start(bf16[384,512]{1,0:T(8,128)(2,1)} %collective-permute-done.1), channel_id=1, source_target_pairs={{0,16},{16,32},{32,48},{48,64},{64,80},{80,96},{96,112},{112,0},{1... | collective-permute-start | bytes 1179656 | tf_op jit(solution)/shard_map/ppermute | solution.py:16
  72.5 28.0 %collective-permute-start.4 = (bf16[384,512]{1,0:T(8,128)(2,1)}, bf16[384,512]{1,0:T(8,128)(2,1)}, u32[]{:S(2)}, u32[]{:S(2)}) collective-permute-start(bf16[384,512]{1,0:T(8,128)(2,1)} %collective-permute-done.2), channel_id=1, source_target_pairs={{0,16},{16,32},{32,48},{48,64},{64,80},{80,96},{96,112},{112,0},{1... | collective-permute-start | bytes 1179656 | tf_op jit(solution)/shard_map/ppermute | solution.py:16
  73.8 28.7 %collective-permute-start.5 = (bf16[384,512]{1,0:T(8,128)(2,1)}, bf16[384,512]{1,0:T(8,128)(2,1)}, u32[]{:S(2)}, u32[]{:S(2)}) collective-permute-start(bf16[384,512]{1,0:T(8,128)(2,1)} %collective-permute-done.3), channel_id=1, source_target_pairs={{0,16},{16,32},{32,48},{48,64},{64,80},{80,96},{96,112},{112,0},{1... | collective-permute-start | bytes 1179656 | tf_op jit(solution)/shard_map/ppermute | solution.py:16
  100.6 28.7 %collective-permute-start.6 = (bf16[384,512]{1,0:T(8,128)(2,1)}, bf16[384,512]{1,0:T(8,128)(2,1)}, u32[]{:S(2)}, u32[]{:S(2)}) collective-permute-start(bf16[384,512]{1,0:T(8,128)(2,1)} %collective-permute-done.4), channel_id=1, source_target_pairs={{0,16},{16,32},{32,48},{48,64},{64,80},{80,96},{96,112},{112,0},{1... | collective-permute-start | bytes 1179656 | tf_op jit(solution)/shard_map/ppermute | solution.py:16
  102.5 27.2 %collective-permute-start.7 = (bf16[384,512]{1,0:T(8,128)(2,1)}, bf16[384,512]{1,0:T(8,128)(2,1)}, u32[]{:S(2)}, u32[]{:S(2)}) collective-permute-start(bf16[384,512]{1,0:T(8,128)(2,1)} %collective-permute-done.5), channel_id=1, source_target_pairs={{0,16},{16,32},{32,48},{48,64},{64,80},{80,96},{96,112},{112,0},{1... | collective-permute-start | bytes 1179656 | tf_op jit(solution)/shard_map/ppermute | solution.py:16
  129.3 27.2 %collective-permute-start.8 = (bf16[384,512]{1,0:T(8,128)(2,1)}, bf16[384,512]{1,0:T(8,128)(2,1)}, u32[]{:S(2)}, u32[]{:S(2)}) collective-permute-start(bf16[384,512]{1,0:T(8,128)(2,1)} %collective-permute-done.6), channel_id=1, source_target_pairs={{0,16},{16,32},{32,48},{48,64},{64,80},{80,96},{96,112},{112,0},{1... | collective-permute-start | bytes 1179656 | tf_op jit(solution)/shard_map/ppermute | solution.py:16
  129.7 27.8 %collective-permute-start.9 = (bf16[384,512]{1,0:T(8,128)(2,1)}, bf16[384,512]{1,0:T(8,128)(2,1)}, u32[]{:S(2)}, u32[]{:S(2)}) collective-permute-start(bf16[384,512]{1,0:T(8,128)(2,1)} %collective-permute-done.7), channel_id=1, source_target_pairs={{0,16},{16,32},{32,48},{48,64},{64,80},{80,96},{96,112},{112,0},{1... | collective-permute-start | bytes 1179656 | tf_op jit(solution)/shard_map/ppermute | solution.py:16
  156.5 27.8 %collective-permute-start.10 = (bf16[384,512]{1,0:T(8,128)(2,1)}, bf16[384,512]{1,0:T(8,128)(2,1)}, u32[]{:S(2)}, u32[]{:S(2)}) collective-permute-start(bf16[384,512]{1,0:T(8,128)(2,1)} %collective-permute-done.8), channel_id=1, source_target_pairs={{0,16},{16,32},{32,48},{48,64},{64,80},{80,96},{96,112},{112,0},{1... | collective-permute-start | bytes 1179656 | tf_op jit(solution)/shard_map/ppermute | solution.py:16
  157.5 28.0 %collective-permute-start.11 = (bf16[384,512]{1,0:T(8,128)(2,1)}, bf16[384,512]{1,0:T(8,128)(2,1)}, u32[]{:S(2)}, u32[]{:S(2)}) collective-permute-start(bf16[384,512]{1,0:T(8,128)(2,1)} %collective-permute-done.9), channel_id=1, source_target_pairs={{0,16},{16,32},{32,48},{48,64},{64,80},{80,96},{96,112},{112,0},{1... | collective-permute-start | bytes 1179656 | tf_op jit(solution)/shard_map/ppermute | solution.py:16
  184.2 27.4 %collective-permute-start.12 = (bf16[384,512]{1,0:T(8,128)(2,1)}, bf16[384,512]{1,0:T(8,128)(2,1)S(1)}, u32[]{:S(2)}, u32[]{:S(2)}) collective-permute-start(bf16[384,512]{1,0:T(8,128)(2,1)} %collective-permute-done.10), channel_id=1, source_target_pairs={{0,16},{16,32},{32,48},{48,64},{64,80},{80,96},{96,112},{112,0},{1... | collective-permute-start | bytes 1179656 | tf_op jit(solution)/shard_map/ppermute | solution.py:16
  185.5 26.1 %collective-permute-start.13 = (bf16[384,512]{1,0:T(8,128)(2,1)}, bf16[384,512]{1,0:T(8,128)(2,1)S(1)}, u32[]{:S(2)}, u32[]{:S(2)}) collective-permute-start(bf16[384,512]{1,0:T(8,128)(2,1)} %collective-permute-done.11), channel_id=1, source_target_pairs={{0,16},{16,32},{32,48},{48,64},{64,80},{80,96},{96,112},{112,0},{1... | collective-permute-start | bytes 1179656 | tf_op jit(solution)/shard_map/ppermute | solution.py:16
  247.6 6.5 %copy-start.11 = (s32[1,1,256]{2,1,0:T(1,128)S(1)}, s32[1,1,256]{2,1,0:T(1,128)}, u32[]{:S(2)}) copy-start(s32[1,1,256]{2,1,0:T(1,128)} %param.33) | copy-start | bytes 3076
  247.6 6.5 %copy-start.10 = (s32[1,1,256]{2,1,0:T(1,128)S(1)}, s32[1,1,256]{2,1,0:T(1,128)}, u32[]{:S(2)}) copy-start(s32[1,1,256]{2,1,0:T(1,128)} %param.31) | copy-start | bytes 3076
  247.6 35.0 %copy-start.12 = (s32[1,1,256]{2,1,0:T(1,128)S(1)}, s32[1,1,256]{2,1,0:T(1,128)}, u32[]{:S(2)}) copy-start(s32[1,1,256]{2,1,0:T(1,128)} %param.32) | copy-start | bytes 3076
  247.6 35.0 %all-to-all-start = ((bf16[16,128,512]{2,1,0:T(8,128)(2,1)}), bf16[16,128,512]{2,1,0:T(8,128)(2,1)}, u32[]{:S(2)}, u32[]{:S(2)}) async-start(bf16[16,128,512]{2,1,0:T(8,128)(2,1)} %broadcast_select_fusion), calls=%async_computation | async-start | bytes 4194304 | tf_op jit(solution)/shard_map/all_to_all | solution.py:98
  285.3 3.8 copy-start.13
  289.0 35.7 %all-to-all-start.1 = ((bf16[16,128,512]{2,1,0:T(8,128)(2,1)}), bf16[16,128,512]{2,1,0:T(8,128)(2,1)}, u32[]{:S(2)}, u32[]{:S(2)}) async-start(bf16[16,128,512]{2,1,0:T(8,128)(2,1)} %bitcast.422), calls=%async_computation.1 | async-start | bytes 4194304 | tf_op jit(solution)/shard_map/all_to_all | solution.py:136
  296.2 303.6 %all-reduce.3.cloned.1.call-start = ((), (), s32[]{:S(2)}) async-start(), calls=%async_computation.2 | async-start | bytes 2097152 | tf_op jit(solution)/shard_map/psum | solution.py:154
  (21 other events, 35.0 us)
Sparse Core Ops, SparseCore 0:
  342.5 257.2 all-reduce.2
where the time goes:
time: 613 us; the launch traced here: 610 us
  waiting for transfers between devices  223 us (36%)
  matrix products  108 us (18%)
  local copies, waits for them, and re-layouts  91.3 us (15%)
  blocking collectives  81.8 us (13%)
  other arithmetic  62.2 us (10%)
  starting transfers between devices  24.7 us (4%)
  between operations  17 us (3%)
    psum x1, waiting for transfers between devices, per_device(): lax.psum((loss_term, loss_part, live_part), ('view', 'seq', 'event'))  172 us
    psum x1, blocking collectives, per_device(): lax.psum((loss_term, loss_part, live_part), ('view', 'seq', 'event'))  81.8 us
    dot_general x24, matrix products, one_group(): jnp.einsum('hqk,khd->hqd', weights.astype(jnp.bfloat16), head_values, pre...  67.5 us
    dynamic_slice x96, local copies, waits for them, and re-layouts, attend(): lax.scan(one_group, state, (key_groups, value_groups, offsets))  41.9 us
    while x66, local copies, waits for them, and re-layouts  34.6 us
    all_to_all x1, waiting for transfers between devices, per_device(): lax.all_to_all(outgoing, ('view', 'seq'), split_axis=0, concat_axis=0, ti...  27.4 us
    reduce_sum x24, other arithmetic, one_group(): total = total * factor + jnp.sum(weights, axis=-1)  24.6 us
    all_to_all x1, waiting for transfers between devices, per_device(): lax.all_to_all(candidate_grads.reshape(senders, capacity, width).astype(j...  24.1 us
  transfers between devices with their start and end apart: 17, of which 3 were waited for; matrix products, arithmetic and copies ran while one was open for 28% of the time, Pallas kernels for 0%

commit v1 on v0

v1 whole, which is shorter than its diff:
```python
import functools

import jax
import jax.numpy as jnp
from jax import lax
from jax.experimental import pallas as pl
from jax.experimental.pallas import tpu as pltpu
from jax.sharding import PartitionSpec as P

HEADS = 16
BLOCK = 128
SHARPNESS_SCALE = 0.07
GROUP = 4
EXTRA = 16
LIST = 32
NEGATIVE = -1e30
LOG2E = 1.4426950408889634

F32 = jnp.float32
BF16 = jnp.bfloat16


def dot(a, b):
    return lax.dot_general(a, b, (((1,), (0,)), ((), ())), preferred_element_type=F32)


def dot_nt(a, b):
    return lax.dot_general(a, b, (((1,), (1,)), ((), ())), preferred_element_type=F32)


def flip(x):
    return jnp.transpose(x, (1, 0))


def pack_kernel(peers, rows, q_ref, k_ref, v_ref, pattern_ref, out_ref):
    width = q_ref.shape[1] // peers
    for at, ref in enumerate((q_ref, k_ref, v_ref)):
        turned = flip(ref[...])
        for j in range(peers):
            out_ref[j, at * width : (at + 1) * width, :] = turned[j * width : (j + 1) * width, :]
    blocks = pattern_ref.shape[1]
    allowed = (pattern_ref[...] > 0).astype(F32)
    before = lax.broadcasted_iota(jnp.int32, (blocks, blocks), 0)
    after = lax.broadcasted_iota(jnp.int32, (blocks, blocks), 1)
    rank = dot(allowed.astype(BF16), (before <= after).astype(BF16)) - 1.0
    place = lax.broadcasted_iota(jnp.int32, (LIST, blocks), 0).astype(F32)
    number = lax.broadcasted_iota(jnp.int32, (LIST, blocks), 1).astype(F32)
    lane = lax.broadcasted_iota(jnp.int32, (LIST, 128), 1)
    table = jnp.zeros((LIST, 128), F32)
    for r in range(rows):
        on = allowed[r : r + 1, :]
        count = jnp.sum(on, axis=1, keepdims=True)
        here = jnp.where(place < count, place, 0.0)
        hit = jnp.where(rank[r : r + 1, :] == here, on, 0.0)
        column = jnp.sum(hit * number, axis=1, keepdims=True)
        column = jnp.where(place[:, :1] == float(blocks), count, column)
        table = jnp.where(lane == r, column, table)
    lists = flip(table)[:EXTRA, :].astype(BF16)
    tail = jnp.concatenate(
        [lists, jnp.zeros((EXTRA, 128 - LIST), BF16)]
        + [jnp.zeros((EXTRA, 128), BF16)] * (q_ref.shape[0] // 128 - 1),
        axis=1,
    )
    for j in range(peers):
        out_ref[j, 3 * width : 3 * width + EXTRA, :] = tail


def pack(queries, keys, values, pattern, peers):
    points, width = queries.shape
    rows = 3 * (width // peers) + EXTRA
    return pl.pallas_call(
        functools.partial(pack_kernel, peers, pattern.shape[0]),
        out_shape=jax.ShapeDtypeStruct((peers, rows, points), BF16),
        in_specs=[pl.BlockSpec(memory_space=pltpu.VMEM)] * 4,
        out_specs=pl.BlockSpec(memory_space=pltpu.VMEM),
        compiler_params=pltpu.CompilerParams(vmem_limit_bytes=32 << 20),
        name="pack_heads",
    )(queries, keys, values, pattern)


def attend_kernel(
    peers, per_peer, table_ref, got_ref, out_ref, qb, kb, vb, item_row, item_step, s_buf, p_buf,
    peak_buf, fade_buf, accum
):
    blocks = peers * per_peer
    head = 32
    factor = head ** (-0.5) * LOG2E
    zero = jnp.zeros((head, BLOCK), BF16)
    ones = (lax.broadcasted_iota(jnp.int32, (EXTRA, BLOCK), 0) == 0).astype(F32).astype(BF16)

    @pl.loop(0, peers)
    def _(j):
        for b in range(per_peer):
            block = j * per_peer + b
            span = slice(b * BLOCK, (b + 1) * BLOCK)
            scaled = got_ref[j, 0 : 2 * head, span].astype(F32) * factor
            high = scaled.astype(BF16)
            low = (scaled - high.astype(F32)).astype(BF16)
            left = jnp.concatenate([high[:head], zero, low[:head], zero], axis=0)
            right = jnp.concatenate([zero, high[head:], zero, low[head:]], axis=0)
            qb[block, :, 0:BLOCK] = left
            qb[block, :, BLOCK : 2 * BLOCK] = right
            turned = got_ref[j, 2 * head : 4 * head, span]
            kb[block, :, :] = flip(jnp.concatenate([turned, turned], axis=0))
            vb[block, 0 : 2 * head, :] = got_ref[j, 4 * head : 6 * head, span]
            vb[block, 2 * head : 2 * head + EXTRA, :] = ones

    vb[blocks, :, :] = jnp.zeros((2 * head + EXTRA, BLOCK), BF16)
    s_buf[...] = jnp.zeros_like(s_buf)
    p_buf[...] = jnp.zeros_like(p_buf)
    peak_buf[...] = jnp.zeros_like(peak_buf)
    fade_buf[...] = jnp.zeros_like(fade_buf)
    accum[...] = jnp.zeros_like(accum)

    def list_row(i, items):
        steps = (table_ref[i, blocks] + GROUP - 1) // GROUP

        def list_step(t, items):
            item_row[items] = i
            item_step[items] = t
            return items + 1

        return lax.fori_loop(0, steps, list_step, items)

    items = lax.fori_loop(0, blocks, list_row, 0)

    def stage(t, best):
        now = lax.rem(t, 2)
        item = jnp.minimum(t, items - 1)
        row, first = item_row[item], item_step[item] * GROUP
        picked = [kb[table_ref[row, first + g]] for g in range(GROUP)]
        scores = dot(jnp.concatenate(picked, axis=0), qb[row])
        peak = jnp.max(scores.reshape(GROUP * BLOCK // 8, 8, 2 * BLOCK), axis=0)
        old_peak = peak_buf[1 - now, 0:1, :]
        item = jnp.clip(t - 1, 0, items - 1)
        best = jnp.where(item_step[item] == 0, NEGATIVE, best)
        new_best = jnp.maximum(best, old_peak)
        weights = jnp.exp2(s_buf[1 - now] - new_best).astype(BF16)
        fade = jnp.exp2(best - new_best)
        item = jnp.clip(t - 2, 0, items - 1)
        row, first = item_row[item], item_step[item] * GROUP
        picked = []
        for g in range(GROUP):
            real = first + g < table_ref[row, blocks]
            picked.append(vb[jnp.where(real, table_ref[row, first + g], blocks)])
        added = dot(jnp.concatenate(picked, axis=1), p_buf[now])
        total = accum[...] * fade_buf[now, 0:1, :] + added
        accum[...] = total
        share = pl.reciprocal(total[2 * head : 2 * head + 1, :])
        j, b = row // per_peer, lax.rem(row, per_peer)
        span = pl.ds(pl.multiple_of(b * BLOCK, BLOCK), BLOCK)
        out_ref[j, 0:head, span] = (total[0:head, 0:BLOCK] * share[:, 0:BLOCK]).astype(BF16)
        out_ref[j, head : 2 * head, span] = (
            total[head : 2 * head, BLOCK : 2 * BLOCK] * share[:, BLOCK : 2 * BLOCK]
        ).astype(BF16)
        p_buf[1 - now] = weights
        fade_buf[1 - now] = jnp.broadcast_to(fade, (8, 2 * BLOCK))
        s_buf[now] = scores
        peak_buf[now] = jnp.broadcast_to(jnp.max(peak, axis=0, keepdims=True), (8, 2 * BLOCK))
        return new_best

    lax.fori_loop(0, items + 2, stage, jnp.full((1, 2 * BLOCK), NEGATIVE, F32))


def attend(table, got, peers):
    points = got.shape[2]
    per_peer = points // BLOCK
    blocks = peers * per_peer
    most = blocks * (-(-blocks // GROUP))
    return pl.pallas_call(
        functools.partial(attend_kernel, peers, per_peer),
        out_shape=jax.ShapeDtypeStruct((peers, 64, points), BF16),
        in_specs=[
            pl.BlockSpec(memory_space=pltpu.SMEM),
            pl.BlockSpec(memory_space=pltpu.VMEM),
        ],
        out_specs=pl.BlockSpec(memory_space=pltpu.VMEM),
        scratch_shapes=[
            pltpu.VMEM((blocks, 128, 2 * BLOCK), BF16),
            pltpu.VMEM((blocks, BLOCK, 128), BF16),
            pltpu.VMEM((blocks + 1, 64 + EXTRA, BLOCK), BF16),
            pltpu.SMEM((most,), jnp.int32),
            pltpu.SMEM((most,), jnp.int32),
            pltpu.VMEM((2, GROUP * BLOCK, 2 * BLOCK), F32),
            pltpu.VMEM((2, GROUP * BLOCK, 2 * BLOCK), BF16),
            pltpu.VMEM((2, 8, 2 * BLOCK), F32),
            pltpu.VMEM((2, 8, 2 * BLOCK), F32),
            pltpu.VMEM((64 + EXTRA, 2 * BLOCK), F32),
        ],
        compiler_params=pltpu.CompilerParams(vmem_limit_bytes=40 << 20),
        name="attend",
    )(table, got)


def hand_out_kernel(turned_ref, served_ref, own_ref, mixed_ref, sent_ref, anchor_ref):
    turned = turned_ref[...]
    points = turned.shape[1]
    mixed_ref[...] = flip(turned)
    requests = served_ref.shape[0]

    def picks(rows):
        at = lax.broadcasted_iota(jnp.int32, (points, rows.shape[1]), 0)
        return (at == rows).astype(F32).astype(BF16)

    for r in range(0, requests, 2):
        both = jnp.concatenate([served_ref[r : r + 1, :], served_ref[r + 1 : r + 2, :]], axis=1)
        found = dot(turned, picks(both)).astype(BF16)
        sent_ref[r] = found[:, :BLOCK]
        sent_ref[r + 1] = found[:, BLOCK:]
    anchor_ref[...] = dot(turned, picks(own_ref[...])).astype(BF16)


def hand_out(turned, served, own_rows):
    width, points = turned.shape
    requests, capacity = served.shape
    anchors = own_rows.shape[1]
    return pl.pallas_call(
        hand_out_kernel,
        out_shape=(
            jax.ShapeDtypeStruct((points, width), BF16),
            jax.ShapeDtypeStruct((requests, width, capacity), BF16),
            jax.ShapeDtypeStruct((width, anchors), BF16),
        ),
        in_specs=[pl.BlockSpec(memory_space=pltpu.VMEM)] * 3,
        out_specs=[pl.BlockSpec(memory_space=pltpu.VMEM)] * 3,
        compiler_params=pltpu.CompilerParams(vmem_limit_bytes=40 << 20),
        name="hand_out",
    )(turned, served, own_rows)


def contrast_kernel(
    cand_ref, anchor_ref, weight_ref, slot_ref, live_ref, grad_ref, sums_ref, embed, unit, inverse,
    logits, grads
):
    pieces, width, capacity = cand_ref.shape
    anchors = anchor_ref.shape[1]
    step = 2
    span = step * capacity
    turned_weight = flip(weight_ref[...])

    def normalise(rows):
        e = dot(turned_weight, rows)
        inv = lax.rsqrt(jnp.sum(e * e, axis=0, keepdims=True) + 1e-06)
        return e, inv, (e * inv).astype(BF16)

    def back(e, inv, g):
        inner = jnp.sum(e * g, axis=0, keepdims=True)
        return (inv * (g - e * (inv * inv * inner))).astype(BF16)

    def rows_of(i):
        return jnp.concatenate([cand_ref[step * i + n] for n in range(step)], axis=1)

    own = anchor_ref[...]
    own_embed, own_inverse, own_unit = normalise(own)
    own_rows = flip(own_unit)

    def column(row):
        return flip(jnp.broadcast_to(row.astype(F32), (128, anchors)))[:, :1]

    slot = column(slot_ref[...])
    live = column(live_ref[...])
    position = lax.broadcasted_iota(jnp.int32, (anchors, span), 1).astype(F32)

    def forward(i, carry):
        total, right = carry
        e, inv, u = normalise(rows_of(i))
        embed[i] = e
        unit[i] = u
        inverse[i] = jnp.broadcast_to(inv, (8, span))
        score = dot(own_rows, u) / SHARPNESS_SCALE
        logits[i] = score
        hit = position == slot - (i * span).astype(F32)
        right = right + jnp.where(hit, score, 0.0)
        return total + jnp.exp(score), right

    nothing = jnp.zeros((anchors, span), F32)
    total, right = lax.fori_loop(0, pieces // step, forward, (nothing, nothing))
    total = jnp.sum(total, axis=1, keepdims=True)
    log_total = jnp.log(total)
    right = jnp.sum(right, axis=1, keepdims=True)
    loss = jnp.sum(live * (log_total - right), axis=0, keepdims=True)
    count = jnp.sum(live, axis=0, keepdims=True)
    row = lax.broadcasted_iota(jnp.int32, (8, 128), 0)
    sums_ref[...] = jnp.where(row == 0, loss, jnp.where(row == 1, count, 0.0))
    share = live / (total * SHARPNESS_SCALE)
    push = live / SHARPNESS_SCALE

    grad_ref[...] = jnp.zeros_like(grad_ref)
    grads[...] = jnp.zeros_like(grads)

    def backward(i, carry):
        hit = position == slot - (i * span).astype(F32)
        d = jnp.exp(logits[i]) * share - jnp.where(hit, push, 0.0)
        d = d.astype(BF16)
        grads[...] += dot_nt(unit[i], d)
        z = back(embed[i], inverse[i, 0:1, :], dot(own_unit, d))
        grad_ref[...] += dot_nt(rows_of(i), z)
        return carry

    lax.fori_loop(0, pieces // step, backward, 0)
    grad_ref[...] += dot_nt(own, back(own_embed, own_inverse, grads[...]))


def contrast(candidates, anchors, weight, slot, live):
    pieces, width, capacity = candidates.shape
    count = anchors.shape[1]
    steps, span = pieces // 2, 2 * capacity
    return pl.pallas_call(
        contrast_kernel,
        out_shape=(
            jax.ShapeDtypeStruct((width, width), F32),
            jax.ShapeDtypeStruct((8, 128), F32),
        ),
        in_specs=[pl.BlockSpec(memory_space=pltpu.VMEM)] * 5,
        out_specs=[pl.BlockSpec(memory_space=pltpu.VMEM)] * 2,
        scratch_shapes=[
            pltpu.VMEM((steps, width, span), F32),
            pltpu.VMEM((steps, width, span), BF16),
            pltpu.VMEM((steps, 8, span), F32),
            pltpu.VMEM((steps, count, span), F32),
            pltpu.VMEM((width, count), F32),
        ],
        compiler_params=pltpu.CompilerParams(vmem_limit_bytes=48 << 20),
        name="contrast",
    )(candidates, anchors, weight, slot, live)


def total_over_devices(grad, sums):
    near, far = ("view", "seq"), "event"
    close, away = lax.axis_size(near), lax.axis_size(far)
    shape = grad.shape
    share = grad.size // close // 128

    def pair(x):
        high = x.astype(BF16)
        low = (x - high.astype(F32)).astype(BF16)
        return jnp.concatenate([high, low], axis=0)

    def split_sum(got):
        summed = jnp.sum(got.astype(F32), axis=0)
        return summed[:share], summed[share : share + 8] + summed[share + 8 :]

    cut = grad.reshape(close, share, 128).astype(BF16)
    both = jnp.concatenate([cut, jnp.broadcast_to(pair(sums)[None], (close, 16, 128))], axis=1)
    part, sums = split_sum(lax.all_to_all(both, near, 0, 0, tiled=True))
    both = jnp.concatenate([part.astype(BF16), pair(sums)], axis=0)
    both = jnp.broadcast_to(both[None], (away,) + both.shape)
    part, sums = split_sum(lax.all_to_all(both, far, 0, 0, tiled=True))
    whole = jnp.broadcast_to(part.astype(BF16)[None], (close, share, 128))
    whole = lax.all_to_all(whole, near, 0, 0, tiled=True)
    return whole.astype(F32).reshape(shape), sums[0, 0] / sums[1, 0]


def per_device(
    query, key, value, pattern, out_weight, served, anchor_rows, positive_slot, anchor_live
):
    points, width = query.shape[2:]
    peers = lax.axis_size("seq")
    rows = pattern.shape[2]
    sent = pack(query[0, 0], key[0, 0], value[0, 0], pattern[0, 0], peers)
    got = lax.all_to_all(sent, "seq", 0, 0, tiled=True)
    part = 3 * (width // peers)
    table = got[:, part : part + rows, :LIST].astype(jnp.int32).reshape(peers * rows, LIST)
    turned = attend(table, got, peers)
    turned = lax.all_to_all(turned, "seq", 0, 0, tiled=True).reshape(width, points)
    mixed, outgoing, anchors = hand_out(turned, served[0, 0], anchor_rows[0])
    incoming = lax.all_to_all(outgoing, ("view", "seq"), 0, 0, tiled=True)
    grad, sums = contrast(incoming, anchors, out_weight, positive_slot[0], anchor_live[0])
    grad_total, loss = total_over_devices(grad, sums)
    return (mixed[None, None], grad_total, loss)


def solution(mesh):
    placed = (
        P("event", "view", "seq", None),
        P("event", "view", "seq", None),
        P("event", "view", "seq", None),
        P("event", "view", "seq", None),
        P(),
        P("event", "view", "seq", None),
        P("event", "view", "seq"),
        P("event", "view", "seq"),
        P("event", "view", "seq"),
    )
    return jax.shard_map(
        per_device,
        mesh=mesh,
        in_specs=placed,
        out_specs=(P("event", "view", "seq", None), P(), P()),
        check_vma=False,
    )
```

time: 613 us -> 175 us (0.29)
  waiting for transfers between devices: 223 us -> 9.49 us
  matrix products: 108 us -> 0 us
  local copies, waits for them, and re-layouts: 91.3 us -> 6.82 us
  other arithmetic: 62.2 us -> 0.31 us
  Pallas kernels: 0 us -> 38.1 us
  blocking collectives: 81.8 us -> 109 us
  starting transfers between devices: 24.7 us -> 6.2 us
  between operations: 17 us -> 3.2 us
    psum x1 -> x0, waiting for transfers between devices: 172 us -> none  [per_device(): lax.psum((loss_term, loss_part, live_part), ('view', 'seq', 'event'))]
    all_to_all x0 -> x5, blocking collectives: none -> 109 us  [the longest x1 34.5 us: per_device(): incoming = lax.all_to_all(outgoing, ('view', 'seq'), 0, 0, tiled=True)]
    dot_general x78 -> x0, matrix products: 108 us -> none  [the longest x24 67.5 us: one_group(): jnp.einsum('hqk,khd->hqd', weights.astype(jnp.bfloat16), head_values, pre...]
    psum x1 -> x0, blocking collectives: 81.8 us -> none  [per_device(): lax.psum((loss_term, loss_part, live_part), ('view', 'seq', 'event'))]
    all_to_all x2 -> x1, waiting for transfers between devices: 51.4 us -> 9.49 us  [total_over_devices(): whole = lax.all_to_all(whole, near, 0, 0, tiled=True)]
    dynamic_slice x96 -> x0, local copies, waits for them, and re-layouts: 41.9 us -> none  [attend(): lax.scan(one_group, state, (key_groups, value_groups, offsets))]
    pallas_call x0 -> x4, Pallas kernels: none -> 38.1 us  [the longest x1 20.9 us: attend(): pl.pallas_call(functools.partial(attend_kernel, peers, per_peer), out_sha...]
    while x66 -> x0, local copies, waits for them, and re-layouts: 34.6 us -> none
  transfers between devices with their start and end apart: 17 -> 1, of which waited for: 3 -> 1; matrix products, arithmetic and copies ran while one was open for 28% -> 0% of each run, Pallas kernels for 0% -> 0%
where the time goes in v1:
time: 175 us; the launch traced here: 173 us
  blocking collectives  109 us (62%)
  Pallas kernels  38.1 us (22%)
  waiting for transfers between devices  9.49 us (5%)
  local copies, waits for them, and re-layouts  6.82 us (4%)
  starting transfers between devices  6.2 us (4%)
  between operations  3.2 us (2%)
    all_to_all x1, blocking collectives, per_device(): incoming = lax.all_to_all(outgoing, ('view', 'seq'), 0, 0, tiled=True)  34.5 us
    all_to_all x1, blocking collectives, total_over_devices(): part, sums = split_sum(lax.all_to_all(both, far, 0, 0, tiled=True))  23.6 us
    all_to_all x1, blocking collectives, per_device(): got = lax.all_to_all(sent, 'seq', 0, 0, tiled=True)  23.4 us
    pallas_call x1, Pallas kernels, attend(): pl.pallas_call(functools.partial(attend_kernel, peers, per_peer), out_sha...  20.9 us
    all_to_all x1, blocking collectives, total_over_devices(): part, sums = split_sum(lax.all_to_all(both, near, 0, 0, tiled=True))  16.4 us
    pallas_call x1, Pallas kernels, contrast(): pl.pallas_call(contrast_kernel, out_shape=(jax.ShapeDtypeStruct((width, w...  14.6 us
    all_to_all x1, blocking collectives, per_device(): lax.all_to_all(turned, 'seq', 0, 0, tiled=True).reshape(width, points)  11.5 us
    all_to_all x1, waiting for transfers between devices, total_over_devices(): whole = lax.all_to_all(whole, near, 0, 0, tiled=True)  9.49 us
  transfers between devices with their start and end apart: 1, of which 1 were waited for; matrix products, arithmetic and copies ran while one was open for 0% of the time, Pallas kernels for 0%

profile of v1, /device:TPU:1, one launch (start us, length us, event | category | flops | bytes accessed | tf_op | source)
XLA Modules:
  0.0 173.5 jit_solution(10871692520695078406)
XLA Ops:
  0.6 0.7 copy.14
  1.3 1.0 copy-done.1
  2.3 1.0 copy-done.2
  3.3 1.0 copy-done.3
  4.3 0.5 pack_heads.1
  4.8 23.4 %all_to_all.30.got_ref = bf16[8,208,384]{2,1,0:T(8,128)(2,1)S(1)} all-to-all(bf16[8,208,384]{2,1,0:T(8,128)(2,1)S(1)} %pack_heads.1), channel_id=1, replica_groups=mesh['view'=2,'seq'=8,'event'=16] {'seq'}, dimensions={0} | all-to-all | bytes 2555904 | tf_op jit(solution)/shard_map/all_to_all | solution.py:361
  28.2 20.9 %attend.1 = bf16[8,64,384]{2,1,0:T(8,128)(2,1)S(1)} custom-call(s32[24,32]{1,0:T(8,128)S(1)} %reshape.32.table_ref, bf16[8,208,384]{2,1,0:T(8,128)(2,1)S(1)} %all_to_all.30.got_ref), custom_call_target="tpu_custom_call" | custom-call | tf_op jit(solution)/shard_map/attend/pallas_call | solution.py:170
  49.2 11.5 %all_to_all.31 = bf16[8,64,384]{2,1,0:T(8,128)(2,1)S(1)} all-to-all(bf16[8,64,384]{2,1,0:T(8,128)(2,1)S(1)} %attend.1), channel_id=1, replica_groups=mesh['view'=2,'seq'=8,'event'=16] {'seq'}, dimensions={0} | all-to-all | bytes 786432 | tf_op jit(solution)/shard_map/all_to_all | solution.py:365
  60.6 0.0 copy-done.7
  60.6 2.1 %hand_out.1 = (bf16[384,512]{1,0:T(8,128)(2,1)}, bf16[16,512,128]{2,1,0:T(8,128)(2,1)S(1)}, bf16[512,256]{1,0:T(8,128)(2,1)S(1)}) custom-call(bf16[512,384]{1,0:T(8,128)(2,1)S(1)} %bitcast.13, s32[16,128]{1,0:T(8,128)S(1)} %bitcast.17, s32[1,256]{1,0:T(1,128)S(1)} %bitcast.21), custom_call_target="tpu_custom_call" | custom-call | tf_op jit(solution)/shard_map/hand_out/pallas_call | solution.py:217
  62.7 34.5 %all_to_all.32.cand_ref = bf16[16,512,128]{2,1,0:T(8,128)(2,1)S(1)} all-to-all(bf16[16,512,128]{2,1,0:T(8,128)(2,1)S(1)} %get-tuple-element.9), channel_id=1, replica_groups=mesh['view'=2,'seq'=8,'event'=16] {'view','seq'}, dimensions={0} | all-to-all | bytes 4194304 | tf_op jit(solution)/shard_map/all_to_all | solution.py:367
  97.2 14.6 %contrast.1 = (f32[512,512]{1,0:T(8,128)S(1)}, f32[8,128]{1,0:T(8,128)S(1)}) custom-call(bf16[16,512,128]{2,1,0:T(8,128)(2,1)S(1)} %all_to_all.32.cand_ref, bf16[512,256]{1,0:T(8,128)(2,1)S(1)} %get-tuple-element.10.anchor_ref, bf16[512,512]{1,0:T(8,128)(2,1)S(1)} %copy-done, s32[1,256]{1,0:T(1,128)S(1)} %bitcast.19, s32[1,256]{1,0:T(1,128)S(1)} %bitcast.20), custom_call_target="tpu_custom_call" | custom-call | tf_op jit(solution)/shard_map/contrast/pallas_call | solution.py:308
  111.8 0.1 convert_element_type.34
  111.9 0.3 convert_element_type.35
  112.3 16.4 %all_to_all.33 = bf16[16,144,128]{2,1,0:T(8,128)(2,1)S(1)} all-to-all(bf16[16,144,128]{2,1,0:T(8,128)(2,1)S(1)} %pad_maximum_fusion), channel_id=1, replica_groups=mesh['view'=2,'seq'=8,'event'=16] {'view','seq'}, dimensions={0} | all-to-all | bytes 1179648 | tf_op jit(solution)/shard_map/all_to_all | solution.py:345
  128.7 0.1 convert_reduce_fusion.1
  128.8 0.1 broadcast_in_dim.10
  128.9 23.6 %all_to_all.34 = bf16[16,144,128]{2,1,0:T(8,128)(2,1)S(1)} all-to-all(bf16[16,144,128]{2,1,0:T(8,128)(2,1)S(1)} %broadcast_in_dim.10), channel_id=1, replica_groups=mesh['view'=2,'seq'=8,'event'=16] {'event'}, dimensions={0} | all-to-all | bytes 1179648 | tf_op jit(solution)/shard_map/all_to_all | solution.py:348
  152.5 0.1 convert_reduce_fusion
  152.6 0.9 broadcast_in_dim.11
  153.5 6.2 %all-to-all-start.5 = ((bf16[16,128,128]{2,1,0:T(8,128)(2,1)}), bf16[16,128,128]{2,1,0:T(8,128)(2,1)S(1)}, u32[]{:S(2)}, u32[]{:S(2)}) async-start(bf16[16,128,128]{2,1,0:T(8,128)(2,1)} %broadcast_in_dim.11), calls=%async_computation.5 | async-start | bytes 1048576 | tf_op jit(solution)/shard_map/all_to_all | solution.py:350
  159.7 0.6 fusion.2
  161.6 9.5 %all-to-all-done.5 = bf16[16,128,128]{2,1,0:T(8,128)(2,1)S(1)} async-done(((bf16[16,128,128]{2,1,0:T(8,128)(2,1)}), bf16[16,128,128]{2,1,0:T(8,128)(2,1)S(1)}, u32[]{:S(2)}, u32[]{:S(2)}) %all-to-all-start.5) | async-done | bytes 524320 | tf_op jit(solution)/shard_map/all_to_all | solution.py:350
  171.1 1.2 reshape.34
  (23 shorter events, 0.1 us)
Async XLA Ops:
  1.3 1.0 copy-start.1
  2.3 1.0 copy-start.2
  3.3 1.0 copy-start.3
  28.2 32.4 %copy-start.4 = (s32[1,1,16,128]{3,2,1,0:T(8,128)S(1)}, s32[1,1,16,128]{3,2,1,0:T(8,128)}, u32[]{:S(2)}) copy-start(s32[1,1,16,128]{3,2,1,0:T(8,128)} %param.14) | copy-start | bytes 24580
  28.2 32.4 %copy-start.7 = (s32[1,1,256]{2,1,0:T(1,128)S(1)}, s32[1,1,256]{2,1,0:T(1,128)}, u32[]{:S(2)}) copy-start(s32[1,1,256]{2,1,0:T(1,128)} %param.15) | copy-start | bytes 3076
  62.7 34.5 %copy-start = (bf16[512,512]{1,0:T(8,128)(2,1)S(1)}, bf16[512,512]{1,0:T(8,128)(2,1)}, u32[]{:S(2)}) copy-start(bf16[512,512]{1,0:T(8,128)(2,1)} %weight_ref.1) | copy-start | bytes 1572868
  62.7 34.5 %copy-start.5 = (s32[1,1,256]{2,1,0:T(1,128)S(1)}, s32[1,1,256]{2,1,0:T(1,128)}, u32[]{:S(2)}) copy-start(s32[1,1,256]{2,1,0:T(1,128)} %param.16) | copy-start | bytes 3076
  62.7 34.5 %copy-start.6 = (s32[1,1,256]{2,1,0:T(1,128)S(1)}, s32[1,1,256]{2,1,0:T(1,128)}, u32[]{:S(2)}) copy-start(s32[1,1,256]{2,1,0:T(1,128)} %param.17) | copy-start | bytes 3076
  153.5 17.6 %all-to-all-start.5 = ((bf16[16,128,128]{2,1,0:T(8,128)(2,1)}), bf16[16,128,128]{2,1,0:T(8,128)(2,1)S(1)}, u32[]{:S(2)}, u32[]{:S(2)}) async-start(bf16[16,128,128]{2,1,0:T(8,128)(2,1)} %broadcast_in_dim.11), calls=%async_computation.5 | async-start | bytes 1048576 | tf_op jit(solution)/shard_map/all_to_all | solution.py:350

commit v2 on v1

v2 whole, which is shorter than its diff:
```python
import functools

import jax
import jax.numpy as jnp
from jax import lax
from jax.experimental import pallas as pl
from jax.experimental.pallas import tpu as pltpu
from jax.sharding import PartitionSpec as P

HEADS = 16
BLOCK = 128
SHARPNESS_SCALE = 0.07
GROUP = 2
ITEMS = 6
EXTRA = 16
EVENT_RUN = 8
LIST = 32
NEGATIVE = -1e30
LOG2E = 1.4426950408889634

F32 = jnp.float32
BF16 = jnp.bfloat16


def dot(a, b):
    return lax.dot_general(a, b, (((1,), (0,)), ((), ())), preferred_element_type=F32)


def dot_nt(a, b):
    return lax.dot_general(a, b, (((1,), (1,)), ((), ())), preferred_element_type=F32)


def flip(x):
    return jnp.transpose(x, (1, 0))


def pack_kernel(
    peers, rows, q_hbm, k_hbm, v_hbm, pattern_hbm, out_ref, q_ref, k_ref, v_ref, pattern_ref, sems
):
    points, full = q_ref.shape
    width = full // peers
    spans = [slice(at, at + BLOCK) for at in range(0, points, BLOCK)]
    copies = [pltpu.make_async_copy(pattern_hbm, pattern_ref, sems.at[0])]
    for n, (source, target) in enumerate(((v_hbm, v_ref), (q_hbm, q_ref), (k_hbm, k_ref))):
        for m, span in enumerate(spans):
            copies.append(
                pltpu.make_async_copy(
                    source.at[span, :], target.at[span, :], sems.at[1 + n * len(spans) + m]
                )
            )
    for copy in copies:
        copy.start()

    copies[0].wait()
    blocks = pattern_ref.shape[1]
    allowed = (pattern_ref[...] > 0).astype(F32)
    before = lax.broadcasted_iota(jnp.int32, (blocks, blocks), 0)
    after = lax.broadcasted_iota(jnp.int32, (blocks, blocks), 1)
    rank = dot(allowed.astype(BF16), (before <= after).astype(BF16)) - 1.0
    place = lax.broadcasted_iota(jnp.int32, (LIST, blocks), 0).astype(F32)
    number = lax.broadcasted_iota(jnp.int32, (LIST, blocks), 1).astype(F32)
    lane = lax.broadcasted_iota(jnp.int32, (LIST, 128), 1)
    table = jnp.zeros((LIST, 128), F32)
    for r in range(rows):
        on = allowed[r : r + 1, :]
        count = jnp.sum(on, axis=1, keepdims=True)
        here = jnp.where(place < count, place, 0.0)
        hit = jnp.where(rank[r : r + 1, :] == here, on, 0.0)
        column = jnp.sum(hit * number, axis=1, keepdims=True)
        column = jnp.where(place[:, :1] == float(blocks), count, column)
        table = jnp.where(lane == r, column, table)
    lists = flip(table)[:EXTRA, :].astype(BF16)
    tail = jnp.concatenate(
        [lists, jnp.zeros((EXTRA, 128 - LIST), BF16)]
        + [jnp.zeros((EXTRA, 128), BF16)] * (points // 128 - 1),
        axis=1,
    )
    for j in range(peers):
        out_ref[j, 3 * width : 3 * width + EXTRA, :] = tail

    for n, (at, ref) in enumerate(((2, v_ref), (0, q_ref))):
        for m, span in enumerate(spans):
            copies[1 + n * len(spans) + m].wait()
            turned = flip(ref[span, :])
            for j in range(peers):
                out_ref[j, at * width : (at + 1) * width, span] = turned[
                    j * width : (j + 1) * width, :
                ]
    for m, span in enumerate(spans):
        copies[1 + 2 * len(spans) + m].wait()
        for j in range(peers):
            cols = slice(j * width, (j + 1) * width)
            first = k_ref[span.start : span.start + width, cols]
            second = k_ref[span.start + width : span.stop, cols]
            out_ref[j, width : 2 * width, span] = jnp.concatenate([first, second], axis=1)


def pack(queries, keys, values, pattern, peers):
    points, width = queries.shape
    rows = 3 * (width // peers) + EXTRA
    return pl.pallas_call(
        functools.partial(pack_kernel, peers, pattern.shape[0]),
        out_shape=jax.ShapeDtypeStruct((peers, rows, points), BF16),
        in_specs=[pl.BlockSpec(memory_space=pl.ANY)] * 4,
        out_specs=pl.BlockSpec(memory_space=pltpu.VMEM),
        scratch_shapes=[
            pltpu.VMEM((points, width), BF16),
            pltpu.VMEM((points, width), BF16),
            pltpu.VMEM((points, width), BF16),
            pltpu.VMEM(pattern.shape, jnp.int32),
            pltpu.SemaphoreType.DMA((1 + 3 * (points // BLOCK),)),
        ],
        compiler_params=pltpu.CompilerParams(vmem_limit_bytes=60 << 20),
        name="pack_heads",
    )(queries, keys, values, pattern)


def four_rows(first, second):
    row = lax.broadcasted_iota(jnp.int32, (8, 128), 0)
    value = jnp.where(lax.rem(row, 2) == 0, first, second)
    high = value.astype(BF16).astype(F32)
    return jnp.where(row < 2, high, jnp.where(row < 4, value - high, 0.0)).astype(BF16)


def attend_kernel(
    peers, per_peer, table_ref, got_ref, out_ref, qb, kb, vb, scored, weighed, peak, fade, accum
):
    blocks = peers * per_peer
    head = 32
    factor = head ** (-0.5) * LOG2E
    zero = jnp.zeros((head, BLOCK), BF16)
    ones = (lax.broadcasted_iota(jnp.int32, (EXTRA, BLOCK), 0) == 0).astype(F32).astype(BF16)

    for j in range(peers):
        for b in range(per_peer):
            block = j * per_peer + b
            span = slice(b * BLOCK, (b + 1) * BLOCK)
            scaled = got_ref[j, 0 : 2 * head, span].astype(F32) * factor
            high = scaled.astype(BF16)
            low = (scaled - high.astype(F32)).astype(BF16)
            left = jnp.concatenate([high[:head], zero, low[:head], zero], axis=0)
            right = jnp.concatenate([zero, high[head:], zero, low[head:]], axis=0)
            qb[block, :, 0:BLOCK] = left
            qb[block, :, BLOCK : 2 * BLOCK] = right
            pair = got_ref[j, 2 * head : 4 * head, span]
            first, second = pair[:, : 2 * head], pair[:, 2 * head :]
            kb[block, : BLOCK // 2, :] = jnp.concatenate([first, first], axis=1)
            kb[block, BLOCK // 2 :, :] = jnp.concatenate([second, second], axis=1)
            vb[block, 0 : 2 * head, :] = got_ref[j, 4 * head : 6 * head, span]
            vb[block, 2 * head : 2 * head + EXTRA, :] = ones

    vb[blocks, :, :] = jnp.zeros((2 * head + EXTRA, BLOCK), BF16)
    for ref in (scored, weighed, peak, fade, accum):
        ref[...] = jnp.zeros_like(ref)

    steps_of = [(table_ref[i, blocks] + GROUP - 1) // GROUP for i in range(blocks)]
    items = functools.reduce(lambda x, y: x + y, steps_of)

    def after(item):
        row, step, real = item
        last = (step + 1) * GROUP >= table_ref[row, blocks]
        end = jnp.logical_and(last, row == blocks - 1)
        return (
            jnp.where(jnp.logical_and(last, row < blocks - 1), row + 1, row),
            jnp.where(end, step, jnp.where(last, 0, step + 1)),
            jnp.where(end, 0, real),
        )

    def turn(t, carry):
        best, at_scores, at_weights, at_sums = carry
        total = accum[...]
        for n, (row, step, real) in enumerate(at_sums):
            first = step * GROUP
            count = jnp.where(real == 1, table_ref[row, blocks], 0)
            picked = []
            for g in range(GROUP):
                picked.append(vb[jnp.where(first + g < count, table_ref[row, first + g], blocks)])
            added = dot(jnp.concatenate(picked, axis=1), weighed[n])
            total = total * fade[n, 0:1, :] + added
            share = pl.reciprocal(total[2 * head : 2 * head + 1, :])
            j, b = row // per_peer, lax.rem(row, per_peer)
            span = pl.ds(pl.multiple_of(b * BLOCK, BLOCK), BLOCK)
            out_ref[j, 0:head, span] = (total[0:head, 0:BLOCK] * share[:, 0:BLOCK]).astype(BF16)
            out_ref[j, head : 2 * head, span] = (
                total[head : 2 * head, BLOCK : 2 * BLOCK] * share[:, BLOCK : 2 * BLOCK]
            ).astype(BF16)
        accum[...] = total
        for n, (row, step, real) in enumerate(at_weights):
            best = jnp.where(jnp.logical_and(step == 0, real == 1), NEGATIVE, best)
            new_best = jnp.maximum(best, peak[n, 0:1, :])
            weighed[n] = jnp.exp2(scored[n] - new_best).astype(BF16)
            fade[n] = jnp.broadcast_to(jnp.exp2(best - new_best), (8, 2 * BLOCK))
            best = new_best
        for n, (row, step, real) in enumerate(at_scores):
            picked = [kb[table_ref[row, step * GROUP + g]] for g in range(GROUP)]
            scores = dot(jnp.concatenate(picked, axis=0), qb[row])
            scored[n] = scores
            top = jnp.max(scores.reshape(GROUP * BLOCK // 8, 8, 2 * BLOCK), axis=0)
            peak[n] = jnp.broadcast_to(jnp.max(top, axis=0, keepdims=True), (8, 2 * BLOCK))
        following = [after(at_scores[-1])]
        for n in range(ITEMS - 1):
            following.append(after(following[-1]))
        return best, tuple(following), at_scores, at_weights

    zero = jnp.int32(0)
    items_at = [(zero, zero, jnp.int32(1))]
    for n in range(ITEMS - 1):
        items_at.append(after(items_at[-1]))
    idle = ((zero, zero, zero),) * ITEMS
    lax.fori_loop(
        0,
        (items + ITEMS - 1) // ITEMS + 2,
        turn,
        (jnp.full((1, 2 * BLOCK), NEGATIVE, F32), tuple(items_at), idle, idle),
    )


def attend(table, got, peers):
    points = got.shape[2]
    per_peer = points // BLOCK
    blocks = peers * per_peer
    return pl.pallas_call(
        functools.partial(attend_kernel, peers, per_peer),
        out_shape=jax.ShapeDtypeStruct((peers, 64, points), BF16),
        in_specs=[
            pl.BlockSpec(memory_space=pltpu.SMEM),
            pl.BlockSpec(memory_space=pltpu.VMEM),
        ],
        out_specs=pl.BlockSpec(memory_space=pltpu.VMEM),
        scratch_shapes=[
            pltpu.VMEM((blocks, 128, 2 * BLOCK), BF16),
            pltpu.VMEM((blocks, BLOCK, 128), BF16),
            pltpu.VMEM((blocks + 1, 64 + EXTRA, BLOCK), BF16),
            pltpu.VMEM((ITEMS, GROUP * BLOCK, 2 * BLOCK), F32),
            pltpu.VMEM((ITEMS, GROUP * BLOCK, 2 * BLOCK), BF16),
            pltpu.VMEM((ITEMS, 8, 2 * BLOCK), F32),
            pltpu.VMEM((ITEMS, 8, 2 * BLOCK), F32),
            pltpu.VMEM((64 + EXTRA, 2 * BLOCK), F32),
        ],
        compiler_params=pltpu.CompilerParams(vmem_limit_bytes=40 << 20),
        name="attend",
    )(table, got)


def hand_out_kernel(turned_ref, served_ref, own_ref, mixed_ref, sent_ref, anchor_ref):
    turned = turned_ref[...]
    points = turned.shape[1]
    mixed_ref[...] = flip(turned)
    requests = served_ref.shape[0]

    def picks(rows):
        at = lax.broadcasted_iota(jnp.int32, (points, rows.shape[1]), 0)
        return (at == rows).astype(F32).astype(BF16)

    for r in range(0, requests, 2):
        both = jnp.concatenate([served_ref[r : r + 1, :], served_ref[r + 1 : r + 2, :]], axis=1)
        found = dot(turned, picks(both)).astype(BF16)
        sent_ref[r] = found[:, :BLOCK]
        sent_ref[r + 1] = found[:, BLOCK:]
    anchor_ref[...] = dot(turned, picks(own_ref[...])).astype(BF16)


def hand_out(turned, served, own_rows):
    width, points = turned.shape
    requests, capacity = served.shape
    anchors = own_rows.shape[1]
    return pl.pallas_call(
        hand_out_kernel,
        out_shape=(
            jax.ShapeDtypeStruct((points, width), BF16),
            jax.ShapeDtypeStruct((requests, width, capacity), BF16),
            jax.ShapeDtypeStruct((width, anchors), BF16),
        ),
        in_specs=[pl.BlockSpec(memory_space=pltpu.VMEM)] * 3,
        out_specs=[pl.BlockSpec(memory_space=pltpu.VMEM)] * 3,
        compiler_params=pltpu.CompilerParams(vmem_limit_bytes=40 << 20),
        name="hand_out",
    )(turned, served, own_rows)


def contrast_kernel(
    cand_ref, anchor_ref, weight_ref, slot_ref, live_ref, out_ref, embed, unit, inverse,
    expo, slopes, pulls
):
    pieces, width, capacity = cand_ref.shape
    anchors = anchor_ref.shape[1]
    span = 2 * capacity
    steps = pieces // 2
    turned_weight = flip(weight_ref[...])

    def normalise(rows):
        e = dot(turned_weight, rows)
        inv = lax.rsqrt(jnp.sum(e * e, axis=0, keepdims=True) + 1e-06)
        return e, inv, (e * inv).astype(BF16)

    def back(e, inv, g):
        inner = jnp.sum(e * g, axis=0, keepdims=True)
        return (inv * g - e * (inv * inv * inv * inner)).astype(BF16)

    def rows_of(i):
        return jnp.concatenate([cand_ref[2 * i], cand_ref[2 * i + 1]], axis=1)

    own = anchor_ref[...]
    own_embed, own_inverse, own_unit = normalise(own)
    own_rows = flip(own_unit)

    def column(row):
        return flip(jnp.broadcast_to(row.astype(F32), (128, anchors)))[:, :1]

    slot = column(slot_ref[...])
    live = column(live_ref[...])
    position = lax.broadcasted_iota(jnp.int32, (anchors, span), 1).astype(F32)
    sharpness = 1.0 / SHARPNESS_SCALE

    total = jnp.zeros((anchors, capacity), F32)
    right = jnp.zeros((anchors, capacity), F32)
    for i in range(steps):
        at = slice(i * span, (i + 1) * span)
        e, inv, u = normalise(rows_of(i))
        embed[:, at] = e
        unit[:, at] = u
        inverse[:, at] = jnp.broadcast_to(inv, (8, span))
        score = dot(own_rows, u)
        hit = position == slot - float(i * span)
        kept = jnp.where(hit, score, 0.0)
        right = right + (kept[:, :capacity] + kept[:, capacity:])
        grown = jnp.exp2(score * (sharpness * LOG2E))
        expo[:, at] = grown
        total = total + (grown[:, :capacity] + grown[:, capacity:])
    total = jnp.sum(total, axis=1, keepdims=True)
    right = jnp.sum(right, axis=1, keepdims=True) * sharpness
    loss = jnp.sum(live * (jnp.log(total) - right), axis=0, keepdims=True)
    count = jnp.sum(live, axis=0, keepdims=True)
    sums = four_rows(loss, count)
    share = live / total * sharpness
    push = live * sharpness

    for i in range(steps):
        at = slice(i * span, (i + 1) * span)
        hit = position == slot - float(i * span)
        d = (expo[:, at] * share - jnp.where(hit, push, 0.0)).astype(BF16)
        slopes[:, at] = d
        pulls[:, at] = back(embed[:, at], inverse[0:1, at], dot(own_unit, d))
    own_pull = back(own_embed, own_inverse, dot_nt(unit[...], slopes[...]))
    taken = jnp.concatenate([cand_ref[n] for n in range(pieces)], axis=1)
    ways = out_ref.shape[0]
    rows = width // ways
    half = width // 2
    for c in range(2):
        grad = dot_nt(taken, pulls[c * half : (c + 1) * half, :])
        grad = (grad + dot_nt(own, own_pull[c * half : (c + 1) * half, :])).astype(BF16)
        for j in range(ways):
            for m in range(half // 128):
                to = (c * (half // 128) + m) * rows
                out_ref[j, to : to + rows, :] = grad[
                    j * rows : (j + 1) * rows, m * 128 : (m + 1) * 128
                ]
    for j in range(ways):
        out_ref[j, rows * width // 128 :, :] = sums


def contrast(candidates, anchors, weight, slot, live, ways):
    pieces, width, capacity = candidates.shape
    count = anchors.shape[1]
    many = pieces * capacity
    return pl.pallas_call(
        contrast_kernel,
        out_shape=jax.ShapeDtypeStruct((ways, width * width // ways // 128 + 8, 128), BF16),
        in_specs=[pl.BlockSpec(memory_space=pltpu.VMEM)] * 5,
        out_specs=pl.BlockSpec(memory_space=pltpu.VMEM),
        scratch_shapes=[
            pltpu.VMEM((width, many), F32),
            pltpu.VMEM((width, many), BF16),
            pltpu.VMEM((8, many), F32),
            pltpu.VMEM((count, many), F32),
            pltpu.VMEM((count, many), BF16),
            pltpu.VMEM((width, many), BF16),
        ],
        compiler_params=pltpu.CompilerParams(vmem_limit_bytes=48 << 20),
        name="contrast",
    )(candidates, anchors, weight, slot, live)


def summed(got_ref):
    total = got_ref[0].astype(F32)
    for n in range(1, got_ref.shape[0]):
        total += got_ref[n].astype(F32)
    part, sums = total[:-8], total[-8:]
    return part, sums[0:1] + sums[2:3], sums[1:2] + sums[3:4]


def first_sum_kernel(got_ref, out_ref):
    part, loss, count = summed(got_ref)
    rows = part.shape[0]
    part = part.astype(BF16)
    sums = four_rows(loss, count)
    for n in range(out_ref.shape[0]):
        out_ref[n, :rows, :] = part
        out_ref[n, rows:, :] = sums


def last_sum_kernel(got_ref, out_ref, loss_ref):
    part, loss, count = summed(got_ref)
    rows = out_ref.shape[1]
    part = part.astype(BF16)
    whole = jnp.concatenate(
        [part[at : at + rows, :] for at in range(0, part.shape[0], rows)], axis=1
    )
    for n in range(out_ref.shape[0]):
        out_ref[n] = whole
    loss_ref[...] = loss / count


def groups():
    close = lax.axis_size(("view", "seq"))
    events = lax.axis_size("event")
    deep = EVENT_RUN if events % EVENT_RUN == 0 else events
    planes = [
        [near * events + far * deep + z for near in range(close) for far in range(events // deep)]
        for z in range(deep)
    ]
    lines = [[far * deep + z for z in range(deep)] for far in range(events // deep)]
    return planes, lines


def total_over_devices(parts, width):
    planes, lines = groups()
    everywhere = ("view", "seq", "event")
    vmem = pl.BlockSpec(memory_space=pltpu.VMEM)
    got = lax.all_to_all(parts, everywhere, 0, 0, axis_index_groups=planes, tiled=True)
    whole = pl.pallas_call(
        first_sum_kernel,
        out_shape=jax.ShapeDtypeStruct((len(lines[0]),) + parts.shape[1:], BF16),
        in_specs=[vmem],
        out_specs=vmem,
        name="first_sum",
    )(got)
    got = lax.all_to_all(whole, "event", 0, 0, axis_index_groups=lines, tiled=True)
    ways = len(planes[0])
    whole, loss = pl.pallas_call(
        last_sum_kernel,
        out_shape=(
            jax.ShapeDtypeStruct((ways, width // ways, width), BF16),
            jax.ShapeDtypeStruct((1, 128), F32),
        ),
        in_specs=[vmem],
        out_specs=[vmem, vmem],
        name="last_sum",
    )(got)
    grad = lax.all_to_all(whole, everywhere, 0, 0, axis_index_groups=planes, tiled=True)
    return grad.reshape(width, width).astype(F32), loss[0, 0]


def per_device(
    query, key, value, pattern, out_weight, served, anchor_rows, positive_slot, anchor_live
):
    points, width = query.shape[2:]
    peers = lax.axis_size("seq")
    rows = pattern.shape[2]
    sent = pack(query[0, 0], key[0, 0], value[0, 0], pattern[0, 0], peers)
    got = lax.all_to_all(sent, "seq", 0, 0, tiled=True)
    part = 3 * (width // peers)
    table = got[:, part : part + rows, :LIST].astype(jnp.int32).reshape(peers * rows, LIST)
    turned = attend(table, got, peers)
    turned = lax.all_to_all(turned, "seq", 0, 0, tiled=True).reshape(width, points)
    mixed, outgoing, anchors = hand_out(turned, served[0, 0], anchor_rows[0])
    incoming = lax.all_to_all(outgoing, ("view", "seq"), 0, 0, tiled=True)
    ways = len(groups()[0][0])
    parts = contrast(incoming, anchors, out_weight, positive_slot[0], anchor_live[0], ways)
    grad_total, loss = total_over_devices(parts, width)
    return (mixed[None, None], grad_total, loss)


def solution(mesh):
    placed = (
        P("event", "view", "seq", None),
        P("event", "view", "seq", None),
        P("event", "view", "seq", None),
        P("event", "view", "seq", None),
        P(),
        P("event", "view", "seq", None),
        P("event", "view", "seq"),
        P("event", "view", "seq"),
        P("event", "view", "seq"),
    )
    return jax.shard_map(
        per_device,
        mesh=mesh,
        in_specs=placed,
        out_specs=(P("event", "view", "seq", None), P(), P()),
        check_vma=False,
    )
```

time: 175 us -> 151 us (0.86)
  blocking collectives: 109 us -> 119 us
  waiting for transfers between devices: 9.49 us -> 0 us
  Pallas kernels: 38.1 us -> 28.8 us
  starting transfers between devices: 6.2 us -> 0 us
  local copies, waits for them, and re-layouts: 6.82 us -> 1.29 us
  between operations: 3.2 us -> 0.67 us
    all_to_all x2 -> x3, blocking collectives: 40 us -> 49.9 us  [the longest x1 17.5 us: total_over_devices(): lax.all_to_all(whole, everywhere, 0, 0, axis_index_groups=planes, tiled=T...]
    all_to_all x1 -> x0, waiting for transfers between devices: 9.49 us -> none  [total_over_devices(): whole = lax.all_to_all(whole, near, 0, 0, tiled=True)]
    pallas_call x1, Pallas kernels: 20.9 us -> 11.6 us  [attend(): pl.pallas_call(functools.partial(attend_kernel, peers, per_peer), out_sha...]
    all_to_all x1 -> x0, starting transfers between devices: 6.2 us -> none  [total_over_devices(): whole = lax.all_to_all(whole, near, 0, 0, tiled=True)]
    pallas_call x1 -> x3, Pallas kernels: 14.6 us -> 12.1 us  [the longest x1 8.54 us: contrast(): pl.pallas_call(contrast_kernel, out_shape=jax.ShapeDtypeStruct((ways, wid...]
    pallas_call x1, Pallas kernels: 0.5 us -> 2.95 us  [pack(): pl.pallas_call(functools.partial(pack_kernel, peers, pattern.shape[0]), o...]
    unnamed x17 -> x11, local copies, waits for them, and re-layouts: 3.69 us -> 1.28 us
  transfers between devices with their start and end apart: 1 -> 0, of which waited for: 1 -> 0; matrix products, arithmetic and copies ran while one was open for 0% -> 0% of each run, Pallas kernels for 0% -> 0%
where the time goes in v2:
time: 151 us
  blocking collectives  119 us (79%)
  Pallas kernels  28.8 us (19%)
    all_to_all x1, blocking collectives, per_device(): incoming = lax.all_to_all(outgoing, ('view', 'seq'), 0, 0, tiled=True)  33.1 us
    all_to_all x1, blocking collectives, per_device(): got = lax.all_to_all(sent, 'seq', 0, 0, tiled=True)  24.3 us
    all_to_all x1, blocking collectives, total_over_devices(): lax.all_to_all(whole, everywhere, 0, 0, axis_index_groups=planes, tiled=T...  17.5 us
    all_to_all x1, blocking collectives, total_over_devices(): lax.all_to_all(whole, 'event', 0, 0, axis_index_groups=lines, tiled=True)  16.4 us
    all_to_all x1, blocking collectives, total_over_devices(): lax.all_to_all(parts, everywhere, 0, 0, axis_index_groups=planes, tiled=T...  16 us
    pallas_call x1, Pallas kernels, attend(): pl.pallas_call(functools.partial(attend_kernel, peers, per_peer), out_sha...  11.6 us
    all_to_all x1, blocking collectives, per_device(): lax.all_to_all(turned, 'seq', 0, 0, tiled=True).reshape(width, points)  11.5 us
    pallas_call x1, Pallas kernels, contrast(): pl.pallas_call(contrast_kernel, out_shape=jax.ShapeDtypeStruct((ways, wid...  8.54 us

profile of v2, /device:TPU:1, one launch (start us, length us, event | category | flops | bytes accessed | tf_op | source)
XLA Modules:
  0.0 150.7 jit_solution(17061597089076807351)
XLA Ops:
  0.6 1.3 copy.14
  1.9 3.0 %pack_heads.1 = bf16[8,208,384]{2,1,0:T(8,128)(2,1)} custom-call(bf16[384,512]{1,0:T(8,128)(2,1)} %bitcast.22, bf16[384,512]{1,0:T(8,128)(2,1)} %bitcast.23, bf16[384,512]{1,0:T(8,128)(2,1)} %bitcast.24, s32[3,24]{1,0:T(4,128)} %bitcast.25), custom_call_target="tpu_custom_call" | custom-call | tf_op jit(solution)/shard_map/pack_heads/pallas_call | solution.py:101
  4.9 24.3 %all_to_all.30.got_ref = bf16[8,208,384]{2,1,0:T(8,128)(2,1)S(1)} all-to-all(bf16[8,208,384]{2,1,0:T(8,128)(2,1)} %pack_heads.1), channel_id=1, replica_groups=mesh['view'=2,'seq'=8,'event'=16] {'seq'}, dimensions={0} | all-to-all | bytes 2555904 | tf_op jit(solution)/shard_map/all_to_all | solution.py:461
  29.2 0.0 copy-start.1
  29.2 0.0 copy-start.2
  29.2 11.6 %attend.1 = bf16[8,64,384]{2,1,0:T(8,128)(2,1)S(1)} custom-call(s32[24,32]{1,0:T(8,128)S(1)} %reshape.21.table_ref, bf16[8,208,384]{2,1,0:T(8,128)(2,1)S(1)} %all_to_all.30.got_ref), custom_call_target="tpu_custom_call" | custom-call | tf_op jit(solution)/shard_map/attend/pallas_call | solution.py:222
  40.8 11.5 %all_to_all.31 = bf16[8,64,384]{2,1,0:T(8,128)(2,1)S(1)} all-to-all(bf16[8,64,384]{2,1,0:T(8,128)(2,1)S(1)} %attend.1), channel_id=1, replica_groups=mesh['view'=2,'seq'=8,'event'=16] {'seq'}, dimensions={0} | all-to-all | bytes 786432 | tf_op jit(solution)/shard_map/all_to_all | solution.py:465
  52.3 0.0 copy-done.1
  52.3 0.0 copy-done.2
  52.3 2.1 %hand_out.1 = (bf16[384,512]{1,0:T(8,128)(2,1)}, bf16[16,512,128]{2,1,0:T(8,128)(2,1)S(1)}, bf16[512,256]{1,0:T(8,128)(2,1)S(1)}) custom-call(bf16[512,384]{1,0:T(8,128)(2,1)S(1)} %bitcast.17, s32[16,128]{1,0:T(8,128)S(1)} %bitcast.18, s32[1,256]{1,0:T(1,128)S(1)} %bitcast.19), custom_call_target="tpu_custom_call" | custom-call | tf_op jit(solution)/shard_map/hand_out/pallas_call | solution.py:267
  54.4 0.0 copy-start
  54.4 0.0 copy-start.3
  54.4 0.0 copy-start.4
  54.4 33.1 %all_to_all.32.cand_ref = bf16[16,512,128]{2,1,0:T(8,128)(2,1)S(1)} all-to-all(bf16[16,512,128]{2,1,0:T(8,128)(2,1)S(1)} %get-tuple-element.9), channel_id=1, replica_groups=mesh['view'=2,'seq'=8,'event'=16] {'view','seq'}, dimensions={0} | all-to-all | bytes 4194304 | tf_op jit(solution)/shard_map/all_to_all | solution.py:467
  87.5 0.0 copy-done
  87.5 0.0 copy-done.3
  87.5 0.0 copy-done.4
  87.5 8.5 %contrast.1 = bf16[32,72,128]{2,1,0:T(8,128)(2,1)S(1)} custom-call(bf16[16,512,128]{2,1,0:T(8,128)(2,1)S(1)} %all_to_all.32.cand_ref, bf16[512,256]{1,0:T(8,128)(2,1)S(1)} %get-tuple-element.10.anchor_ref, bf16[512,512]{1,0:T(8,128)(2,1)S(1)} %copy-done, s32[1,256]{1,0:T(1,128)S(1)} %bitcast.20, s32[1,256]{1,0:T(1,128)S(1)} %bitcast.21), custom_call_target="tpu_custom_call" | custom-call | tf_op jit(solution)/shard_map/contrast/pallas_call | solution.py:366
  96.1 16.0 %all_to_all.33.got_ref = bf16[32,72,128]{2,1,0:T(8,128)(2,1)} all-to-all(bf16[32,72,128]{2,1,0:T(8,128)(2,1)S(1)} %contrast.1), channel_id=1, replica_groups={{0,8,16,24,32,40,48,56,64,72,80,88,96,104,112,120,128,136,144,152,160,1..., dimensions={0} | all-to-all | bytes 1179648 | tf_op jit(solution)/shard_map/all_to_all | solution.py:430
  112.1 1.8 %first_sum.1 = bf16[8,72,128]{2,1,0:T(8,128)(2,1)} custom-call(bf16[32,72,128]{2,1,0:T(8,128)(2,1)} %all_to_all.33.got_ref), custom_call_target="tpu_custom_call" | custom-call | tf_op jit(solution)/shard_map/first_sum/pallas_call | solution.py:431
  113.9 16.4 %all_to_all.34.got_ref = bf16[8,72,128]{2,1,0:T(8,128)(2,1)} all-to-all(bf16[8,72,128]{2,1,0:T(8,128)(2,1)} %first_sum.1), channel_id=1, replica_groups={{0,1,2,3,4,5,6,7},{8,9,10,11,12,13,14,15},{16,17,18,19,20,21,22,23},{24..., dimensions={0} | all-to-all | bytes 294912 | tf_op jit(solution)/shard_map/all_to_all | solution.py:438
  130.3 1.8 %last_sum.1 = (bf16[32,16,512]{2,1,0:T(8,128)(2,1)}, f32[1,128]{1,0:T(1,128)}) custom-call(bf16[8,72,128]{2,1,0:T(8,128)(2,1)} %all_to_all.34.got_ref), custom_call_target="tpu_custom_call" | custom-call | tf_op jit(solution)/shard_map/last_sum/pallas_call | solution.py:440
  132.1 17.5 %all_to_all.35 = bf16[32,16,512]{2,1,0:T(8,128)(2,1)S(1)} all-to-all(bf16[32,16,512]{2,1,0:T(8,128)(2,1)} %get-tuple-element.11), channel_id=1, replica_groups={{0,8,16,24,32,40,48,56,64,72,80,88,96,104,112,120,128,136,144,152,160,1..., dimensions={0} | all-to-all | bytes 1048576 | tf_op jit(solution)/shard_map/all_to_all | solution.py:450
  149.6 1.1 bitcast_convert_fusion
  (2 shorter events, 0.0 us)
Async XLA Ops:
  29.2 23.1 %copy-start.1 = (s32[1,1,16,128]{3,2,1,0:T(8,128)S(1)}, s32[1,1,16,128]{3,2,1,0:T(8,128)}, u32[]{:S(2)}) copy-start(s32[1,1,16,128]{3,2,1,0:T(8,128)} %param.14) | copy-start | bytes 24580
  29.2 23.1 %copy-start.2 = (s32[1,1,256]{2,1,0:T(1,128)S(1)}, s32[1,1,256]{2,1,0:T(1,128)}, u32[]{:S(2)}) copy-start(s32[1,1,256]{2,1,0:T(1,128)} %param.15) | copy-start | bytes 3076
  54.4 33.1 %copy-start = (bf16[512,512]{1,0:T(8,128)(2,1)S(1)}, bf16[512,512]{1,0:T(8,128)(2,1)}, u32[]{:S(2)}) copy-start(bf16[512,512]{1,0:T(8,128)(2,1)} %weight_ref.1) | copy-start | bytes 1572868
  54.4 33.1 %copy-start.3 = (s32[1,1,256]{2,1,0:T(1,128)S(1)}, s32[1,1,256]{2,1,0:T(1,128)}, u32[]{:S(2)}) copy-start(s32[1,1,256]{2,1,0:T(1,128)} %param.16) | copy-start | bytes 3076
  54.4 33.1 %copy-start.4 = (s32[1,1,256]{2,1,0:T(1,128)S(1)}, s32[1,1,256]{2,1,0:T(1,128)}, u32[]{:S(2)}) copy-start(s32[1,1,256]{2,1,0:T(1,128)} %param.17) | copy-start | bytes 3076

commit v3 on v2

--- a/solution.py
+++ b/solution.py
@@ -12,7 +12,8 @@
 SHARPNESS_SCALE = 0.07
 GROUP = 2
 ITEMS = 6
-EXTRA = 16
+EXTRA = 8
+ONES = 16
 EVENT_RUN = 8
 LIST = 32
 NEGATIVE = -1e30
@@ -52,8 +53,9 @@
         copy.start()
 
     copies[0].wait()
-    blocks = pattern_ref.shape[1]
-    allowed = (pattern_ref[...] > 0).astype(F32)
+    blocks = pattern_ref.shape[2]
+    allowed = jnp.concatenate([pattern_ref[r] for r in range(rows)], axis=0)
+    allowed = (allowed > 0).astype(F32)
     before = lax.broadcasted_iota(jnp.int32, (blocks, blocks), 0)
     after = lax.broadcasted_iota(jnp.int32, (blocks, blocks), 1)
     rank = dot(allowed.astype(BF16), (before <= after).astype(BF16)) - 1.0
@@ -129,7 +131,7 @@
     head = 32
     factor = head ** (-0.5) * LOG2E
     zero = jnp.zeros((head, BLOCK), BF16)
-    ones = (lax.broadcasted_iota(jnp.int32, (EXTRA, BLOCK), 0) == 0).astype(F32).astype(BF16)
+    ones = (lax.broadcasted_iota(jnp.int32, (ONES, BLOCK), 0) == 0).astype(F32).astype(BF16)
 
     for j in range(peers):
         for b in range(per_peer):
@@ -147,9 +149,9 @@
             kb[block, : BLOCK // 2, :] = jnp.concatenate([first, first], axis=1)
             kb[block, BLOCK // 2 :, :] = jnp.concatenate([second, second], axis=1)
             vb[block, 0 : 2 * head, :] = got_ref[j, 4 * head : 6 * head, span]
-            vb[block, 2 * head : 2 * head + EXTRA, :] = ones
-
-    vb[blocks, :, :] = jnp.zeros((2 * head + EXTRA, BLOCK), BF16)
+            vb[block, 2 * head : 2 * head + ONES, :] = ones
+
+    vb[blocks, :, :] = jnp.zeros((2 * head + ONES, BLOCK), BF16)
     for ref in (scored, weighed, peak, fade, accum):
         ref[...] = jnp.zeros_like(ref)
 
@@ -230,12 +232,12 @@
         scratch_shapes=[
             pltpu.VMEM((blocks, 128, 2 * BLOCK), BF16),
             pltpu.VMEM((blocks, BLOCK, 128), BF16),
-            pltpu.VMEM((blocks + 1, 64 + EXTRA, BLOCK), BF16),
+            pltpu.VMEM((blocks + 1, 64 + ONES, BLOCK), BF16),
             pltpu.VMEM((ITEMS, GROUP * BLOCK, 2 * BLOCK), F32),
             pltpu.VMEM((ITEMS, GROUP * BLOCK, 2 * BLOCK), BF16),
             pltpu.VMEM((ITEMS, 8, 2 * BLOCK), F32),
             pltpu.VMEM((ITEMS, 8, 2 * BLOCK), F32),
-            pltpu.VMEM((64 + EXTRA, 2 * BLOCK), F32),
+            pltpu.VMEM((64 + ONES, 2 * BLOCK), F32),
         ],
         compiler_params=pltpu.CompilerParams(vmem_limit_bytes=40 << 20),
         name="attend",
@@ -279,8 +281,8 @@
 
 
 def contrast_kernel(
-    cand_ref, anchor_ref, weight_ref, slot_ref, live_ref, out_ref, embed, unit, inverse,
-    expo, slopes, pulls
+    cand_ref, anchor_ref, weight_ref, slot_ref, live_ref, away_ref, kept_ref, embed, unit, inverse,
+    expo, slopes, pulls, own_pulls
 ):
     pieces, width, capacity = cand_ref.shape
     anchors = anchor_ref.shape[1]
@@ -341,33 +343,34 @@
         d = (expo[:, at] * share - jnp.where(hit, push, 0.0)).astype(BF16)
         slopes[:, at] = d
         pulls[:, at] = back(embed[:, at], inverse[0:1, at], dot(own_unit, d))
-    own_pull = back(own_embed, own_inverse, dot_nt(unit[...], slopes[...]))
+    own_pulls[...] = back(own_embed, own_inverse, dot_nt(unit[...], slopes[...]))
     taken = jnp.concatenate([cand_ref[n] for n in range(pieces)], axis=1)
-    ways = out_ref.shape[0]
+    ways = kept_ref.shape[0]
     rows = width // ways
     half = width // 2
-    for c in range(2):
-        grad = dot_nt(taken, pulls[c * half : (c + 1) * half, :])
-        grad = (grad + dot_nt(own, own_pull[c * half : (c + 1) * half, :])).astype(BF16)
+    core = lax.rem(lax.axis_index("seq"), 2)
+    for out_ref, mine in ((away_ref, 1 - core), (kept_ref, core)):
+        at = pl.ds(pl.multiple_of(mine * half, half), half)
+        grad = dot_nt(taken, pulls[at, :])
+        grad = (grad + dot_nt(own, own_pulls[at, :])).astype(BF16)
         for j in range(ways):
             for m in range(half // 128):
-                to = (c * (half // 128) + m) * rows
-                out_ref[j, to : to + rows, :] = grad[
+                out_ref[j, m * rows : (m + 1) * rows, :] = grad[
                     j * rows : (j + 1) * rows, m * 128 : (m + 1) * 128
                 ]
-    for j in range(ways):
-        out_ref[j, rows * width // 128 :, :] = sums
+            out_ref[j, rows * half // 128 :, :] = sums
 
 
 def contrast(candidates, anchors, weight, slot, live, ways):
     pieces, width, capacity = candidates.shape
     count = anchors.shape[1]
     many = pieces * capacity
+    half = jax.ShapeDtypeStruct((ways, width * width // 2 // ways // 128 + 8, 128), BF16)
     return pl.pallas_call(
         contrast_kernel,
-        out_shape=jax.ShapeDtypeStruct((ways, width * width // ways // 128 + 8, 128), BF16),
+        out_shape=(half,) * 2,
         in_specs=[pl.BlockSpec(memory_space=pltpu.VMEM)] * 5,
-        out_specs=pl.BlockSpec(memory_space=pltpu.VMEM),
+        out_specs=[pl.BlockSpec(memory_space=pltpu.VMEM)] * 2,
         scratch_shapes=[
             pltpu.VMEM((width, many), F32),
             pltpu.VMEM((width, many), BF16),
@@ -375,6 +378,7 @@
             pltpu.VMEM((count, many), F32),
             pltpu.VMEM((count, many), BF16),
             pltpu.VMEM((width, many), BF16),
+            pltpu.VMEM((width, count), BF16),
         ],
         compiler_params=pltpu.CompilerParams(vmem_limit_bytes=48 << 20),
         name="contrast",
@@ -411,44 +415,81 @@
     loss_ref[...] = loss / count
 
 
+def core_sum_kernel(one_ref, two_ref, out_ref):
+    rows = out_ref.shape[1] - 8
+    total = one_ref[:, :rows, :].astype(F32) + two_ref[:, :rows, :].astype(F32)
+    sums = one_ref[0, rows:, :].astype(F32) + two_ref[0, rows:, :].astype(F32)
+    sums = four_rows(sums[0:1] + sums[2:3], sums[1:2] + sums[3:4])
+    out_ref[:, :rows, :] = total.astype(BF16)
+    for n in range(out_ref.shape[0]):
+        out_ref[n, rows:, :] = sums
+
+
 def groups():
     close = lax.axis_size(("view", "seq"))
     events = lax.axis_size("event")
     deep = EVENT_RUN if events % EVENT_RUN == 0 else events
     planes = [
-        [near * events + far * deep + z for near in range(close) for far in range(events // deep)]
+        [
+            near * events + far * deep + z
+            for near in range(core, close, 2)
+            for far in range(events // deep)
+        ]
+        for core in range(2)
         for z in range(deep)
     ]
     lines = [[far * deep + z for z in range(deep)] for far in range(events // deep)]
     return planes, lines
 
 
-def total_over_devices(parts, width):
+def to_other_core(x):
+    peers = lax.axis_size("seq")
+    return lax.ppermute(x, "seq", [(i, i ^ 1) for i in range(peers)])
+
+
+def small(kernel, name, out_shape, *operands):
+    vmem = pl.BlockSpec(memory_space=pltpu.VMEM)
+    return pl.pallas_call(
+        kernel,
+        out_shape=out_shape,
+        in_specs=[vmem] * len(operands),
+        out_specs=jax.tree.map(lambda shape: vmem, out_shape),
+        compiler_params=pltpu.CompilerParams(vmem_limit_bytes=12 << 20),
+        name=name,
+    )(*operands)
+
+
+def total_over_devices(away, kept, core, width):
     planes, lines = groups()
     everywhere = ("view", "seq", "event")
-    vmem = pl.BlockSpec(memory_space=pltpu.VMEM)
+    ways, half = len(planes[0]), width // 2
+    shape = kept.shape
+    parts = small(
+        core_sum_kernel, "core_sum", jax.ShapeDtypeStruct(shape, BF16), kept, to_other_core(away)
+    )
     got = lax.all_to_all(parts, everywhere, 0, 0, axis_index_groups=planes, tiled=True)
-    whole = pl.pallas_call(
-        first_sum_kernel,
-        out_shape=jax.ShapeDtypeStruct((len(lines[0]),) + parts.shape[1:], BF16),
-        in_specs=[vmem],
-        out_specs=vmem,
-        name="first_sum",
-    )(got)
+    whole = small(
+        first_sum_kernel, "first_sum", jax.ShapeDtypeStruct((len(lines[0]),) + shape[1:], BF16), got
+    )
     got = lax.all_to_all(whole, "event", 0, 0, axis_index_groups=lines, tiled=True)
-    ways = len(planes[0])
-    whole, loss = pl.pallas_call(
+    whole, loss = small(
         last_sum_kernel,
-        out_shape=(
-            jax.ShapeDtypeStruct((ways, width // ways, width), BF16),
+        "last_sum",
+        (
+            jax.ShapeDtypeStruct((ways, width // ways, half), BF16),
             jax.ShapeDtypeStruct((1, 128), F32),
         ),
-        in_specs=[vmem],
-        out_specs=[vmem, vmem],
-        name="last_sum",
-    )(got)
-    grad = lax.all_to_all(whole, everywhere, 0, 0, axis_index_groups=planes, tiled=True)
-    return grad.reshape(width, width).astype(F32), loss[0, 0]
+        got,
+    )
+    mine = lax.all_to_all(whole, everywhere, 0, 0, axis_index_groups=planes, tiled=True)
+    mine = mine.reshape(width, half)
+    other = to_other_core(mine)
+    grad = jnp.where(
+        core == 0,
+        jnp.concatenate([mine, other], axis=1),
+        jnp.concatenate([other, mine], axis=1),
+    )
+    return grad.astype(F32), loss[0, 0]
 
 
 def per_device(
@@ -457,7 +498,8 @@
     points, width = query.shape[2:]
     peers = lax.axis_size("seq")
     rows = pattern.shape[2]
-    sent = pack(query[0, 0], key[0, 0], value[0, 0], pattern[0, 0], peers)
+    sent = pack(query[0, 0], key[0, 0], value[0, 0], pattern[0, 0][:, None, :], peers)
+    sent, core = lax.optimization_barrier((sent, lax.rem(lax.axis_index("seq"), 2)))
     got = lax.all_to_all(sent, "seq", 0, 0, tiled=True)
     part = 3 * (width // peers)
     table = got[:, part : part + rows, :LIST].astype(jnp.int32).reshape(peers * rows, LIST)
@@ -466,8 +508,10 @@
     mixed, outgoing, anchors = hand_out(turned, served[0, 0], anchor_rows[0])
     incoming = lax.all_to_all(outgoing, ("view", "seq"), 0, 0, tiled=True)
     ways = len(groups()[0][0])
-    parts = contrast(incoming, anchors, out_weight, positive_slot[0], anchor_live[0], ways)
-    grad_total, loss = total_over_devices(parts, width)
+    away, kept = contrast(
+        incoming, anchors, out_weight, positive_slot[0], anchor_live[0], ways
+    )
+    grad_total, loss = total_over_devices(away, kept, core, width)
     return (mixed[None, None], grad_total, loss)
 
 

time: 151 us -> 142 us (0.940)
  blocking collectives: 119 us -> 108 us
  starting transfers between devices: 0 us -> 5.14 us
  Pallas kernels: 28.8 us -> 24.4 us
  waiting for transfers between devices: 0 us -> 2.37 us
    all_to_all x1, blocking collectives: 17.5 us -> 10.6 us  [total_over_devices(): lax.all_to_all(whole, everywhere, 0, 0, axis_index_groups=planes, tiled=T...]
    ppermute x0 -> x2, starting transfers between devices: none -> 5.14 us  [to_other_core(): return lax.ppermute(x, 'seq', [(i, i ^ 1) for i in range(peers)])]
    all_to_all x1, blocking collectives: 16 us -> 11.1 us  [total_over_devices(): lax.all_to_all(parts, everywhere, 0, 0, axis_index_groups=planes, tiled=T...]
    pallas_call x3 -> x4, Pallas kernels: 12.1 us -> 9.51 us  [the longest x1 8.83 us: contrast(): pl.pallas_call(contrast_kernel, out_shape=(half,) * 2, in_specs=[pl.Block...]
    ppermute x0 -> x2, waiting for transfers between devices: none -> 2.37 us  [to_other_core(): return lax.ppermute(x, 'seq', [(i, i ^ 1) for i in range(peers)])]
    pallas_call x1, Pallas kernels: 11.6 us -> 9.93 us  [attend(): pl.pallas_call(functools.partial(attend_kernel, peers, per_peer), out_sha...]
  transfers between devices with their start and end apart: 0 -> 2, of which waited for: 0 -> 2; matrix products, arithmetic and copies ran while one was open for 0% -> 0% of each run, Pallas kernels for 0% -> 0%
where the time goes in v3:
time: 142 us
  blocking collectives  108 us (76%)
  Pallas kernels  24.4 us (17%)
  starting transfers between devices  5.14 us (4%)
  waiting for transfers between devices  2.37 us (2%)
    all_to_all x1, blocking collectives, per_device(): incoming = lax.all_to_all(outgoing, ('view', 'seq'), 0, 0, tiled=True)  33.6 us
    all_to_all x1, blocking collectives, per_device(): got = lax.all_to_all(sent, 'seq', 0, 0, tiled=True)  23.8 us
    all_to_all x1, blocking collectives, total_over_devices(): lax.all_to_all(whole, 'event', 0, 0, axis_index_groups=lines, tiled=True)  17.7 us
    all_to_all x1, blocking collectives, per_device(): lax.all_to_all(turned, 'seq', 0, 0, tiled=True).reshape(width, points)  11.4 us
    all_to_all x1, blocking collectives, total_over_devices(): lax.all_to_all(parts, everywhere, 0, 0, axis_index_groups=planes, tiled=T...  11.1 us
    all_to_all x1, blocking collectives, total_over_devices(): lax.all_to_all(whole, everywhere, 0, 0, axis_index_groups=planes, tiled=T...  10.6 us
    pallas_call x1, Pallas kernels, attend(): pl.pallas_call(functools.partial(attend_kernel, peers, per_peer), out_sha...  9.93 us
    pallas_call x1, Pallas kernels, contrast(): pl.pallas_call(contrast_kernel, out_shape=(half,) * 2, in_specs=[pl.Block...  8.83 us
  transfers between devices with their start and end apart: 2, of which 2 were waited for; matrix products, arithmetic and copies ran while one was open for 0% of the time, Pallas kernels for 0%

profile of v3, /device:TPU:1, one launch (start us, length us, event | category | flops | bytes accessed | tf_op | source)
XLA Modules:
  0.0 142.0 jit_solution(12537381089474381309)
XLA Ops:
  0.6 2.9 %pack_heads.1 = bf16[8,200,384]{2,1,0:T(8,128)(2,1)} custom-call(bf16[384,512]{1,0:T(8,128)(2,1)} %bitcast.20, bf16[384,512]{1,0:T(8,128)(2,1)} %bitcast.21, bf16[384,512]{1,0:T(8,128)(2,1)} %bitcast.22, s32[3,1,24]{2,1,0:T(1,128)} %bitcast.23), custom_call_target="tpu_custom_call" | custom-call | tf_op jit(solution)/shard_map/pack_heads/pallas_call | solution.py:103
  3.6 23.8 %all_to_all.30.got_ref = bf16[8,200,384]{2,1,0:T(8,128)(2,1)S(1)} all-to-all(bf16[8,200,384]{2,1,0:T(8,128)(2,1)} %pack_heads.1), channel_id=1, replica_groups=mesh['view'=2,'seq'=8,'event'=16] {'seq'}, dimensions={0} | all-to-all | bytes 2457600 | tf_op jit(solution)/shard_map/all_to_all | solution.py:503
  27.4 0.0 copy-start.4
  27.5 9.9 %attend.1 = bf16[8,64,384]{2,1,0:T(8,128)(2,1)S(1)} custom-call(s32[24,32]{1,0:T(8,128)S(1)} %reshape.22.table_ref, bf16[8,200,384]{2,1,0:T(8,128)(2,1)S(1)} %all_to_all.30.got_ref), custom_call_target="tpu_custom_call" | custom-call | tf_op jit(solution)/shard_map/attend/pallas_call | solution.py:224
  37.4 11.4 %all_to_all.31 = bf16[8,64,384]{2,1,0:T(8,128)(2,1)S(1)} all-to-all(bf16[8,64,384]{2,1,0:T(8,128)(2,1)S(1)} %attend.1), channel_id=1, replica_groups=mesh['view'=2,'seq'=8,'event'=16] {'seq'}, dimensions={0} | all-to-all | bytes 786432 | tf_op jit(solution)/shard_map/all_to_all | solution.py:507
  48.8 0.0 copy-done.1
  48.8 0.0 copy-done.4
  48.8 2.1 %hand_out.1 = (bf16[384,512]{1,0:T(8,128)(2,1)}, bf16[16,512,128]{2,1,0:T(8,128)(2,1)S(1)}, bf16[512,256]{1,0:T(8,128)(2,1)S(1)}) custom-call(bf16[512,384]{1,0:T(8,128)(2,1)S(1)} %bitcast.13, s32[16,128]{1,0:T(8,128)S(1)} %bitcast.14, s32[1,256]{1,0:T(1,128)S(1)} %bitcast.17), custom_call_target="tpu_custom_call" | custom-call | tf_op jit(solution)/shard_map/hand_out/pallas_call | solution.py:269
  50.9 33.6 %all_to_all.32.cand_ref = bf16[16,512,128]{2,1,0:T(8,128)(2,1)S(1)} all-to-all(bf16[16,512,128]{2,1,0:T(8,128)(2,1)S(1)} %get-tuple-element.15), channel_id=1, replica_groups=mesh['view'=2,'seq'=8,'event'=16] {'view','seq'}, dimensions={0} | all-to-all | bytes 4194304 | tf_op jit(solution)/shard_map/all_to_all | solution.py:509
  84.4 0.0 copy-done
  84.4 0.0 copy-done.2
  84.4 0.0 copy-done.3
  84.5 8.8 %contrast.1 = (bf16[16,72,128]{2,1,0:T(8,128)(2,1)S(1)}, bf16[16,72,128]{2,1,0:T(8,128)(2,1)S(1)}) custom-call(bf16[16,512,128]{2,1,0:T(8,128)(2,1)S(1)} %all_to_all.32.cand_ref, bf16[512,256]{1,0:T(8,128)(2,1)S(1)} %get-tuple-element.16.anchor_ref, bf16[512,512]{1,0:T(8,128)(2,1)S(1)} %copy-done, s32[1,256]{1,0:T(1,128)S(1)} %bitcast.15, s32[1,256]{1,0:T(1,128)S(1)} %bitcast.16), custom_call_target="tpu_custom_call" | custom-call | tf_op jit(solution)/shard_map/contrast/pallas_call | solution.py:369
  93.3 1.3 collective-permute-start
  94.6 1.2 collective-permute-done.two_ref
  95.8 0.1 core_sum.1
  95.8 11.1 %all_to_all.33.got_ref = bf16[16,72,128]{2,1,0:T(8,128)(2,1)S(1)} all-to-all(bf16[16,72,128]{2,1,0:T(8,128)(2,1)S(1)} %core_sum.1), channel_id=1, replica_groups={{0,8,32,40,64,72,96,104,128,136,160,168,192,200,224,232},{1,9,33,41,65,..., dimensions={0} | all-to-all | bytes 589824 | tf_op jit(solution)/shard_map/all_to_all | solution.py:470
  106.9 0.1 first_sum.1
  107.0 17.7 %all_to_all.34.got_ref = bf16[8,72,128]{2,1,0:T(8,128)(2,1)S(1)} all-to-all(bf16[8,72,128]{2,1,0:T(8,128)(2,1)S(1)} %first_sum.1), channel_id=1, replica_groups={{0,1,2,3,4,5,6,7},{8,9,10,11,12,13,14,15},{16,17,18,19,20,21,22,23},{24..., dimensions={0} | all-to-all | bytes 294912 | tf_op jit(solution)/shard_map/all_to_all | solution.py:474
  124.7 0.5 last_sum.1
  125.2 10.6 %all_to_all.35 = bf16[16,32,256]{2,1,0:T(8,128)(2,1)S(1)} all-to-all(bf16[16,32,256]{2,1,0:T(8,128)(2,1)S(1)} %get-tuple-element.19), channel_id=1, replica_groups={{0,8,32,40,64,72,96,104,128,136,160,168,192,200,224,232},{1,9,33,41,65,..., dimensions={0} | all-to-all | bytes 524288 | tf_op jit(solution)/shard_map/all_to_all | solution.py:484
  135.8 3.9 %collective-permute-start.1 = (bf16[512,256]{1,0:T(8,128)(2,1)S(1)}, bf16[512,256]{1,0:T(8,128)(2,1)S(1)}, u32[]{:S(2)}, u32[]{:S(2)}) collective-permute-start(bf16[512,256]{1,0:T(8,128)(2,1)S(1)} %bitcast.18), channel_id=1, source_target_pairs={{0,16},{16,0},{32,48},{48,32},{64,80},{80,64},{96,112},{112,96},{1... | collective-permute-start | bytes 786440 | tf_op jit(solution)/shard_map/ppermute | solution.py:447
  139.7 1.2 collective-permute-done.1
  140.9 1.1 fusion
  (6 shorter events, 0.0 us)
Async XLA Ops:
  27.4 21.4 %copy-start.1 = (s32[1,1,16,128]{3,2,1,0:T(8,128)S(1)}, s32[1,1,16,128]{3,2,1,0:T(8,128)}, u32[]{:S(2)}) copy-start(s32[1,1,16,128]{3,2,1,0:T(8,128)} %param.14) | copy-start | bytes 24580
  27.4 21.4 %copy-start.4 = (s32[1,1,256]{2,1,0:T(1,128)S(1)}, s32[1,1,256]{2,1,0:T(1,128)}, u32[]{:S(2)}) copy-start(s32[1,1,256]{2,1,0:T(1,128)} %param.15) | copy-start | bytes 3076
  50.8 33.6 %copy-start = (bf16[512,512]{1,0:T(8,128)(2,1)S(1)}, bf16[512,512]{1,0:T(8,128)(2,1)}, u32[]{:S(2)}) copy-start(bf16[512,512]{1,0:T(8,128)(2,1)} %weight_ref.1) | copy-start | bytes 1572868
  50.8 33.6 %copy-start.2 = (s32[1,1,256]{2,1,0:T(1,128)S(1)}, s32[1,1,256]{2,1,0:T(1,128)}, u32[]{:S(2)}) copy-start(s32[1,1,256]{2,1,0:T(1,128)} %param.16) | copy-start | bytes 3076
  50.8 33.6 %copy-start.3 = (s32[1,1,256]{2,1,0:T(1,128)S(1)}, s32[1,1,256]{2,1,0:T(1,128)}, u32[]{:S(2)}) copy-start(s32[1,1,256]{2,1,0:T(1,128)} %param.17) | copy-start | bytes 3076
  93.3 2.5 %collective-permute-start = (bf16[16,72,128]{2,1,0:T(8,128)(2,1)S(1)}, bf16[16,72,128]{2,1,0:T(8,128)(2,1)S(1)}, u32[]{:S(2)}, u32[]{:S(2)}) collective-permute-start(bf16[16,72,128]{2,1,0:T(8,128)(2,1)S(1)} %get-tuple-element.18), channel_id=1, source_target_pairs={{0,16},{16,0},{32,48},{48,32},{64,80},{80,64},{96,112},{112,96},{1... | collective-permute-start | bytes 884744 | tf_op jit(solution)/shard_map/ppermute | solution.py:447
  135.8 5.0 %collective-permute-start.1 = (bf16[512,256]{1,0:T(8,128)(2,1)S(1)}, bf16[512,256]{1,0:T(8,128)(2,1)S(1)}, u32[]{:S(2)}, u32[]{:S(2)}) collective-permute-start(bf16[512,256]{1,0:T(8,128)(2,1)S(1)} %bitcast.18), channel_id=1, source_target_pairs={{0,16},{16,0},{32,48},{48,32},{64,80},{80,64},{96,112},{112,96},{1... | collective-permute-start | bytes 786440 | tf_op jit(solution)/shard_map/ppermute | solution.py:447

commit v4 on v3

--- a/solution.py
+++ b/solution.py
@@ -103,7 +103,7 @@
     return pl.pallas_call(
         functools.partial(pack_kernel, peers, pattern.shape[0]),
         out_shape=jax.ShapeDtypeStruct((peers, rows, points), BF16),
-        in_specs=[pl.BlockSpec(memory_space=pl.ANY)] * 4,
+        in_specs=[pl.BlockSpec(memory_space=pltpu.HBM)] * 4,
         out_specs=pl.BlockSpec(memory_space=pltpu.VMEM),
         scratch_shapes=[
             pltpu.VMEM((points, width), BF16),
@@ -112,9 +112,9 @@
             pltpu.VMEM(pattern.shape, jnp.int32),
             pltpu.SemaphoreType.DMA((1 + 3 * (points // BLOCK),)),
         ],
-        compiler_params=pltpu.CompilerParams(vmem_limit_bytes=60 << 20),
+        compiler_params=pltpu.CompilerParams(vmem_limit_bytes=16 << 20),
         name="pack_heads",
-    )(queries, keys, values, pattern)
+    )(*(pltpu.with_memory_space_constraint(x, pltpu.HBM) for x in (queries, keys, values, pattern)))
 
 
 def four_rows(first, second):
@@ -152,9 +152,6 @@
             vb[block, 2 * head : 2 * head + ONES, :] = ones
 
     vb[blocks, :, :] = jnp.zeros((2 * head + ONES, BLOCK), BF16)
-    for ref in (scored, weighed, peak, fade, accum):
-        ref[...] = jnp.zeros_like(ref)
-
     steps_of = [(table_ref[i, blocks] + GROUP - 1) // GROUP for i in range(blocks)]
     items = functools.reduce(lambda x, y: x + y, steps_of)
 
@@ -170,7 +167,7 @@
 
     def turn(t, carry):
         best, at_scores, at_weights, at_sums = carry
-        total = accum[...]
+        total = jnp.where(t < 3, 0.0, accum[...])
         for n, (row, step, real) in enumerate(at_sums):
             first = step * GROUP
             count = jnp.where(real == 1, table_ref[row, blocks], 0)
@@ -316,19 +313,32 @@
 
     total = jnp.zeros((anchors, capacity), F32)
     right = jnp.zeros((anchors, capacity), F32)
-    for i in range(steps):
+    def take(i, e):
         at = slice(i * span, (i + 1) * span)
-        e, inv, u = normalise(rows_of(i))
+        inv = lax.rsqrt(jnp.sum(e * e, axis=0, keepdims=True) + 1e-06)
         embed[:, at] = e
-        unit[:, at] = u
+        unit[:, at] = (e * inv).astype(BF16)
         inverse[:, at] = jnp.broadcast_to(inv, (8, span))
-        score = dot(own_rows, u)
+
+    def judge(i, score, total, right):
+        at = slice(i * span, (i + 1) * span)
         hit = position == slot - float(i * span)
         kept = jnp.where(hit, score, 0.0)
         right = right + (kept[:, :capacity] + kept[:, capacity:])
         grown = jnp.exp2(score * (sharpness * LOG2E))
         expo[:, at] = grown
-        total = total + (grown[:, :capacity] + grown[:, capacity:])
+        return total + (grown[:, :capacity] + grown[:, capacity:]), right
+
+    e = dot(turned_weight, rows_of(0))
+    for i in range(steps):
+        following = dot(turned_weight, rows_of(i + 1)) if i + 1 < steps else None
+        take(i, e)
+        e = following
+        if i > 0:
+            score = dot(own_rows, unit[:, (i - 1) * span : i * span])
+            total, right = judge(i - 1, score, total, right)
+    score = dot(own_rows, unit[:, (steps - 1) * span :])
+    total, right = judge(steps - 1, score, total, right)
     total = jnp.sum(total, axis=1, keepdims=True)
     right = jnp.sum(right, axis=1, keepdims=True) * sharpness
     loss = jnp.sum(live * (jnp.log(total) - right), axis=0, keepdims=True)
@@ -337,13 +347,22 @@
     share = live / total * sharpness
     push = live * sharpness
 
-    for i in range(steps):
+    def slope(i):
         at = slice(i * span, (i + 1) * span)
         hit = position == slot - float(i * span)
         d = (expo[:, at] * share - jnp.where(hit, push, 0.0)).astype(BF16)
         slopes[:, at] = d
-        pulls[:, at] = back(embed[:, at], inverse[0:1, at], dot(own_unit, d))
-    own_pulls[...] = back(own_embed, own_inverse, dot_nt(unit[...], slopes[...]))
+        return dot(own_unit, d)
+
+    g = slope(0)
+    for i in range(steps):
+        at = slice(i * span, (i + 1) * span)
+        following = slope(i + 1) if i + 1 < steps else None
+        part = dot_nt(unit[:, at], slopes[:, at])
+        own_grads = part if i == 0 else own_grads + part
+        pulls[:, at] = back(embed[:, at], inverse[0:1, at], g)
+        g = following
+    own_pulls[...] = back(own_embed, own_inverse, own_grads)
     taken = jnp.concatenate([cand_ref[n] for n in range(pieces)], axis=1)
     ways = kept_ref.shape[0]
     rows = width // ways

time: 142 us -> 138 us (0.972)
  Pallas kernels: 24.4 us -> 20.1 us
    pallas_call x1, Pallas kernels: 8.83 us -> 6.24 us  [contrast(): pl.pallas_call(contrast_kernel, out_shape=(half,) * 2, in_specs=[pl.Block...]
where the time goes in v4:
time: 138 us
  blocking collectives  108 us (78%)
  Pallas kernels  20.1 us (15%)
  starting transfers between devices  5.13 us (4%)
  waiting for transfers between devices  2.37 us (2%)
    all_to_all x1, blocking collectives, per_device(): incoming = lax.all_to_all(outgoing, ('view', 'seq'), 0, 0, tiled=True)  34.8 us
    all_to_all x1, blocking collectives, per_device(): got = lax.all_to_all(sent, 'seq', 0, 0, tiled=True)  22.9 us
    all_to_all x1, blocking collectives, total_over_devices(): lax.all_to_all(whole, 'event', 0, 0, axis_index_groups=lines, tiled=True)  17.6 us
    all_to_all x1, blocking collectives, per_device(): lax.all_to_all(turned, 'seq', 0, 0, tiled=True).reshape(width, points)  11.4 us
    all_to_all x1, blocking collectives, total_over_devices(): lax.all_to_all(parts, everywhere, 0, 0, axis_index_groups=planes, tiled=T...  11.1 us
    all_to_all x1, blocking collectives, total_over_devices(): lax.all_to_all(whole, everywhere, 0, 0, axis_index_groups=planes, tiled=T...  10.6 us
    pallas_call x1, Pallas kernels, attend(): pl.pallas_call(functools.partial(attend_kernel, peers, per_peer), out_sha...  9.29 us
    pallas_call x1, Pallas kernels, contrast(): pl.pallas_call(contrast_kernel, out_shape=(half,) * 2, in_specs=[pl.Block...  6.24 us
  transfers between devices with their start and end apart: 2, of which 2 were waited for; matrix products, arithmetic and copies ran while one was open for 0% of the time, Pallas kernels for 0%

profile of v4, /device:TPU:1, one launch (start us, length us, event | category | flops | bytes accessed | tf_op | source)
XLA Modules:
  0.0 137.9 jit_solution(761326083819151979)
XLA Ops:
  0.6 1.9 %pack_heads.1 = bf16[8,200,384]{2,1,0:T(8,128)(2,1)S(1)} custom-call(bf16[384,512]{1,0:T(8,128)(2,1)} %bitcast.20, bf16[384,512]{1,0:T(8,128)(2,1)} %bitcast.21, bf16[384,512]{1,0:T(8,128)(2,1)} %bitcast.22, s32[3,1,24]{2,1,0:T(1,128)} %bitcast.23), custom_call_target="tpu_custom_call" | custom-call | tf_op jit(solution)/shard_map/pack_heads/pallas_call | solution.py:103
  2.5 22.9 %all_to_all.30.got_ref = bf16[8,200,384]{2,1,0:T(8,128)(2,1)S(1)} all-to-all(bf16[8,200,384]{2,1,0:T(8,128)(2,1)S(1)} %pack_heads.1), channel_id=1, replica_groups=mesh['view'=2,'seq'=8,'event'=16] {'seq'}, dimensions={0} | all-to-all | bytes 2457600 | tf_op jit(solution)/shard_map/all_to_all | solution.py:522
  25.4 0.0 copy-start.4
  25.5 9.3 %attend.1 = bf16[8,64,384]{2,1,0:T(8,128)(2,1)S(1)} custom-call(s32[24,32]{1,0:T(8,128)S(1)} %reshape.22.table_ref, bf16[8,200,384]{2,1,0:T(8,128)(2,1)S(1)} %all_to_all.30.got_ref), custom_call_target="tpu_custom_call" | custom-call | tf_op jit(solution)/shard_map/attend/pallas_call | solution.py:221
  34.8 11.4 %all_to_all.31 = bf16[8,64,384]{2,1,0:T(8,128)(2,1)S(1)} all-to-all(bf16[8,64,384]{2,1,0:T(8,128)(2,1)S(1)} %attend.1), channel_id=1, replica_groups=mesh['view'=2,'seq'=8,'event'=16] {'seq'}, dimensions={0} | all-to-all | bytes 786432 | tf_op jit(solution)/shard_map/all_to_all | solution.py:526
  46.2 0.0 copy-done.1
  46.2 0.0 copy-done.4
  46.2 2.1 %hand_out.1 = (bf16[384,512]{1,0:T(8,128)(2,1)}, bf16[16,512,128]{2,1,0:T(8,128)(2,1)S(1)}, bf16[512,256]{1,0:T(8,128)(2,1)S(1)}) custom-call(bf16[512,384]{1,0:T(8,128)(2,1)S(1)} %bitcast.13, s32[16,128]{1,0:T(8,128)S(1)} %bitcast.14, s32[1,256]{1,0:T(1,128)S(1)} %bitcast.17), custom_call_target="tpu_custom_call" | custom-call | tf_op jit(solution)/shard_map/hand_out/pallas_call | solution.py:266
  48.2 34.8 %all_to_all.32.cand_ref = bf16[16,512,128]{2,1,0:T(8,128)(2,1)S(1)} all-to-all(bf16[16,512,128]{2,1,0:T(8,128)(2,1)S(1)} %get-tuple-element.15), channel_id=1, replica_groups=mesh['view'=2,'seq'=8,'event'=16] {'view','seq'}, dimensions={0} | all-to-all | bytes 4194304 | tf_op jit(solution)/shard_map/all_to_all | solution.py:528
  83.0 0.0 copy-done
  83.1 0.0 copy-done.2
  83.1 0.0 copy-done.3
  83.1 6.2 %contrast.1 = (bf16[16,72,128]{2,1,0:T(8,128)(2,1)S(1)}, bf16[16,72,128]{2,1,0:T(8,128)(2,1)S(1)}) custom-call(bf16[16,512,128]{2,1,0:T(8,128)(2,1)S(1)} %all_to_all.32.cand_ref, bf16[512,256]{1,0:T(8,128)(2,1)S(1)} %get-tuple-element.16.anchor_ref, bf16[512,512]{1,0:T(8,128)(2,1)S(1)} %copy-done, s32[1,256]{1,0:T(1,128)S(1)} %bitcast.15, s32[1,256]{1,0:T(1,128)S(1)} %bitcast.16), custom_call_target="tpu_custom_call" | custom-call | tf_op jit(solution)/shard_map/contrast/pallas_call | solution.py:388
  89.3 1.3 collective-permute-start
  90.6 1.2 collective-permute-done.two_ref
  91.8 0.1 core_sum.1
  91.8 11.1 %all_to_all.33.got_ref = bf16[16,72,128]{2,1,0:T(8,128)(2,1)S(1)} all-to-all(bf16[16,72,128]{2,1,0:T(8,128)(2,1)S(1)} %core_sum.1), channel_id=1, replica_groups={{0,8,32,40,64,72,96,104,128,136,160,168,192,200,224,232},{1,9,33,41,65,..., dimensions={0} | all-to-all | bytes 589824 | tf_op jit(solution)/shard_map/all_to_all | solution.py:489
  102.9 0.1 first_sum.1
  103.0 17.6 %all_to_all.34.got_ref = bf16[8,72,128]{2,1,0:T(8,128)(2,1)S(1)} all-to-all(bf16[8,72,128]{2,1,0:T(8,128)(2,1)S(1)} %first_sum.1), channel_id=1, replica_groups={{0,1,2,3,4,5,6,7},{8,9,10,11,12,13,14,15},{16,17,18,19,20,21,22,23},{24..., dimensions={0} | all-to-all | bytes 294912 | tf_op jit(solution)/shard_map/all_to_all | solution.py:493
  120.6 0.5 last_sum.1
  121.1 10.6 %all_to_all.35 = bf16[16,32,256]{2,1,0:T(8,128)(2,1)S(1)} all-to-all(bf16[16,32,256]{2,1,0:T(8,128)(2,1)S(1)} %get-tuple-element.19), channel_id=1, replica_groups={{0,8,32,40,64,72,96,104,128,136,160,168,192,200,224,232},{1,9,33,41,65,..., dimensions={0} | all-to-all | bytes 524288 | tf_op jit(solution)/shard_map/all_to_all | solution.py:503
  131.7 3.9 %collective-permute-start.1 = (bf16[512,256]{1,0:T(8,128)(2,1)S(1)}, bf16[512,256]{1,0:T(8,128)(2,1)S(1)}, u32[]{:S(2)}, u32[]{:S(2)}) collective-permute-start(bf16[512,256]{1,0:T(8,128)(2,1)S(1)} %bitcast.18), channel_id=1, source_target_pairs={{0,16},{16,0},{32,48},{48,32},{64,80},{80,64},{96,112},{112,96},{1... | collective-permute-start | bytes 786440 | tf_op jit(solution)/shard_map/ppermute | solution.py:466
  135.6 1.2 collective-permute-done.1
  136.8 1.1 fusion
  (6 shorter events, 0.0 us)
Async XLA Ops:
  25.4 20.7 %copy-start.1 = (s32[1,1,16,128]{3,2,1,0:T(8,128)S(1)}, s32[1,1,16,128]{3,2,1,0:T(8,128)}, u32[]{:S(2)}) copy-start(s32[1,1,16,128]{3,2,1,0:T(8,128)} %param.14) | copy-start | bytes 24580
  25.4 20.7 %copy-start.4 = (s32[1,1,256]{2,1,0:T(1,128)S(1)}, s32[1,1,256]{2,1,0:T(1,128)}, u32[]{:S(2)}) copy-start(s32[1,1,256]{2,1,0:T(1,128)} %param.15) | copy-start | bytes 3076
  48.2 34.8 %copy-start = (bf16[512,512]{1,0:T(8,128)(2,1)S(1)}, bf16[512,512]{1,0:T(8,128)(2,1)}, u32[]{:S(2)}) copy-start(bf16[512,512]{1,0:T(8,128)(2,1)} %weight_ref.1) | copy-start | bytes 1572868
  48.2 34.8 %copy-start.2 = (s32[1,1,256]{2,1,0:T(1,128)S(1)}, s32[1,1,256]{2,1,0:T(1,128)}, u32[]{:S(2)}) copy-start(s32[1,1,256]{2,1,0:T(1,128)} %param.16) | copy-start | bytes 3076
  48.2 34.8 %copy-start.3 = (s32[1,1,256]{2,1,0:T(1,128)S(1)}, s32[1,1,256]{2,1,0:T(1,128)}, u32[]{:S(2)}) copy-start(s32[1,1,256]{2,1,0:T(1,128)} %param.17) | copy-start | bytes 3076
  89.3 2.5 %collective-permute-start = (bf16[16,72,128]{2,1,0:T(8,128)(2,1)S(1)}, bf16[16,72,128]{2,1,0:T(8,128)(2,1)S(1)}, u32[]{:S(2)}, u32[]{:S(2)}) collective-permute-start(bf16[16,72,128]{2,1,0:T(8,128)(2,1)S(1)} %get-tuple-element.18), channel_id=1, source_target_pairs={{0,16},{16,0},{32,48},{48,32},{64,80},{80,64},{96,112},{112,96},{1... | collective-permute-start | bytes 884744 | tf_op jit(solution)/shard_map/ppermute | solution.py:466
  131.7 5.0 %collective-permute-start.1 = (bf16[512,256]{1,0:T(8,128)(2,1)S(1)}, bf16[512,256]{1,0:T(8,128)(2,1)S(1)}, u32[]{:S(2)}, u32[]{:S(2)}) collective-permute-start(bf16[512,256]{1,0:T(8,128)(2,1)S(1)} %bitcast.18), channel_id=1, source_target_pairs={{0,16},{16,0},{32,48},{48,32},{64,80},{80,64},{96,112},{112,96},{1... | collective-permute-start | bytes 786440 | tf_op jit(solution)/shard_map/ppermute | solution.py:466

commit v5 on v4

--- a/solution.py
+++ b/solution.py
@@ -241,10 +241,14 @@
     )(table, got)
 
 
-def hand_out_kernel(turned_ref, served_ref, own_ref, mixed_ref, sent_ref, anchor_ref):
+def hand_out_kernel(
+    turned_ref, served_ref, own_ref, mixed_hbm, sent_ref, anchor_ref, mixed_ref, sem
+):
     turned = turned_ref[...]
     points = turned.shape[1]
     mixed_ref[...] = flip(turned)
+    leaving = pltpu.make_async_copy(mixed_ref, mixed_hbm, sem.at[0])
+    leaving.start()
     requests = served_ref.shape[0]
 
     def picks(rows):
@@ -257,6 +261,7 @@
         sent_ref[r] = found[:, :BLOCK]
         sent_ref[r + 1] = found[:, BLOCK:]
     anchor_ref[...] = dot(turned, picks(own_ref[...])).astype(BF16)
+    leaving.wait()
 
 
 def hand_out(turned, served, own_rows):
@@ -271,15 +276,21 @@
             jax.ShapeDtypeStruct((width, anchors), BF16),
         ),
         in_specs=[pl.BlockSpec(memory_space=pltpu.VMEM)] * 3,
-        out_specs=[pl.BlockSpec(memory_space=pltpu.VMEM)] * 3,
+        out_specs=[
+            pl.BlockSpec(memory_space=pl.ANY),
+            pl.BlockSpec(memory_space=pltpu.VMEM),
+            pl.BlockSpec(memory_space=pltpu.VMEM),
+        ],
+        scratch_shapes=[pltpu.VMEM((points, width), BF16), pltpu.SemaphoreType.DMA((1,))],
         compiler_params=pltpu.CompilerParams(vmem_limit_bytes=40 << 20),
         name="hand_out",
     )(turned, served, own_rows)
 
 
 def contrast_kernel(
-    cand_ref, anchor_ref, weight_ref, slot_ref, live_ref, away_ref, kept_ref, embed, unit, inverse,
-    expo, slopes, pulls, own_pulls
+    cand_ref, anchor_ref, weight_ref, slot_ref, live_ref, away_ref, pulls,
+    own_pulls, embed, unit, inverse,
+    expo, slopes
 ):
     pieces, width, capacity = cand_ref.shape
     anchors = anchor_ref.shape[1]
@@ -363,21 +374,46 @@
         pulls[:, at] = back(embed[:, at], inverse[0:1, at], g)
         g = following
     own_pulls[...] = back(own_embed, own_inverse, own_grads)
+    core = lax.rem(lax.axis_index("seq"), 2)
+    half_of_gradient(1 - core, cand_ref, own, pulls, own_pulls, sums, away_ref)
+
+
+def half_of_gradient(mine, cand_ref, own, pulls, own_pulls, sums, out_ref):
+    pieces, width = cand_ref.shape[:2]
+    ways = out_ref.shape[0]
+    rows, half = width // ways, width // 2
     taken = jnp.concatenate([cand_ref[n] for n in range(pieces)], axis=1)
-    ways = kept_ref.shape[0]
-    rows = width // ways
-    half = width // 2
+    at = pl.ds(pl.multiple_of(mine * half, half), half)
+    grad = dot_nt(taken, pulls[at, :])
+    grad = (grad + dot_nt(own, own_pulls[at, :])).astype(BF16)
+    for j in range(ways):
+        for m in range(half // 128):
+            out_ref[j, m * rows : (m + 1) * rows, :] = grad[
+                j * rows : (j + 1) * rows, m * 128 : (m + 1) * 128
+            ]
+        out_ref[j, rows * half // 128 :, :] = sums
+
+
+def keep_kernel(cand_ref, anchor_ref, pulls_ref, own_pulls_ref, away_ref, kept_ref):
     core = lax.rem(lax.axis_index("seq"), 2)
-    for out_ref, mine in ((away_ref, 1 - core), (kept_ref, core)):
-        at = pl.ds(pl.multiple_of(mine * half, half), half)
-        grad = dot_nt(taken, pulls[at, :])
-        grad = (grad + dot_nt(own, own_pulls[at, :])).astype(BF16)
-        for j in range(ways):
-            for m in range(half // 128):
-                out_ref[j, m * rows : (m + 1) * rows, :] = grad[
-                    j * rows : (j + 1) * rows, m * 128 : (m + 1) * 128
-                ]
-            out_ref[j, rows * half // 128 :, :] = sums
+    sums = away_ref[0, away_ref.shape[1] - 8 :, :]
+    half_of_gradient(core, cand_ref, anchor_ref[...], pulls_ref, own_pulls_ref, sums, kept_ref)
+
+
+def keep(candidates, anchors, pulls, own_pulls, away):
+    vmem = pl.BlockSpec(memory_space=pltpu.VMEM)
+    width, many = pulls.shape
+    return pl.pallas_call(
+        keep_kernel,
+        out_shape=jax.ShapeDtypeStruct(away.shape, BF16),
+        in_specs=[vmem] * 5,
+        out_specs=vmem,
+        compiler_params=pltpu.CompilerParams(vmem_limit_bytes=16 << 20),
+        cost_estimate=pl.CostEstimate(
+            flops=width * width * many, bytes_accessed=4 * width * many, transcendentals=0
+        ),
+        name="keep",
+    )(candidates, anchors, pulls, own_pulls, away)
 
 
 def contrast(candidates, anchors, weight, slot, live, ways):
@@ -387,19 +423,21 @@
     half = jax.ShapeDtypeStruct((ways, width * width // 2 // ways // 128 + 8, 128), BF16)
     return pl.pallas_call(
         contrast_kernel,
-        out_shape=(half,) * 2,
+        out_shape=(
+            half,
+            jax.ShapeDtypeStruct((width, many), BF16),
+            jax.ShapeDtypeStruct((width, count), BF16),
+        ),
         in_specs=[pl.BlockSpec(memory_space=pltpu.VMEM)] * 5,
-        out_specs=[pl.BlockSpec(memory_space=pltpu.VMEM)] * 2,
+        out_specs=[pl.BlockSpec(memory_space=pltpu.VMEM)] * 3,
         scratch_shapes=[
             pltpu.VMEM((width, many), F32),
             pltpu.VMEM((width, many), BF16),
             pltpu.VMEM((8, many), F32),
             pltpu.VMEM((count, many), F32),
             pltpu.VMEM((count, many), BF16),
-            pltpu.VMEM((width, many), BF16),
-            pltpu.VMEM((width, count), BF16),
         ],
-        compiler_params=pltpu.CompilerParams(vmem_limit_bytes=48 << 20),
+        compiler_params=pltpu.CompilerParams(vmem_limit_bytes=28 << 20),
         name="contrast",
     )(candidates, anchors, weight, slot, live)
 
@@ -478,13 +516,13 @@
     )(*operands)
 
 
-def total_over_devices(away, kept, core, width):
+def total_over_devices(received, kept, core, width):
     planes, lines = groups()
     everywhere = ("view", "seq", "event")
     ways, half = len(planes[0]), width // 2
     shape = kept.shape
     parts = small(
-        core_sum_kernel, "core_sum", jax.ShapeDtypeStruct(shape, BF16), kept, to_other_core(away)
+        core_sum_kernel, "core_sum", jax.ShapeDtypeStruct(shape, BF16), kept, received
     )
     got = lax.all_to_all(parts, everywhere, 0, 0, axis_index_groups=planes, tiled=True)
     whole = small(
@@ -527,10 +565,12 @@
     mixed, outgoing, anchors = hand_out(turned, served[0, 0], anchor_rows[0])
     incoming = lax.all_to_all(outgoing, ("view", "seq"), 0, 0, tiled=True)
     ways = len(groups()[0][0])
-    away, kept = contrast(
+    away, pulls, own_pulls = contrast(
         incoming, anchors, out_weight, positive_slot[0], anchor_live[0], ways
     )
-    grad_total, loss = total_over_devices(away, kept, core, width)
+    received = to_other_core(away)
+    kept = keep(incoming, anchors, pulls, own_pulls, away)
+    grad_total, loss = total_over_devices(received, kept, core, width)
     return (mixed[None, None], grad_total, loss)
 
 

time: 138 us -> 137 us (level)
  Pallas kernels: 20.1 us -> 22.2 us
  blocking collectives: 108 us -> 106 us
    all_to_all x1, blocking collectives: 17.6 us -> 14.2 us  [total_over_devices(): lax.all_to_all(whole, 'event', 0, 0, axis_index_groups=lines, tiled=True)]
    pallas_call x1 -> x2, Pallas kernels: 6.24 us -> 7.36 us  [the longest x1 6.54 us: contrast(): pl.pallas_call(contrast_kernel, out_shape=(half, jax.ShapeDtypeStruct((wi...]
  transfers between devices with their start and end apart: 2 -> 2, of which waited for: 2 -> 2; matrix products, arithmetic and copies ran while one was open for 0% -> 0% of each run, Pallas kernels for 0% -> 1%
where the time goes in v5:
time: 137 us; the launch traced here: 136 us
  blocking collectives  106 us (77%)
  Pallas kernels  22.2 us (16%)
  starting transfers between devices  5.13 us (4%)
  waiting for transfers between devices  1.55 us (1%)
    all_to_all x1, blocking collectives, per_device(): incoming = lax.all_to_all(outgoing, ('view', 'seq'), 0, 0, tiled=True)  35.3 us
    all_to_all x1, blocking collectives, per_device(): got = lax.all_to_all(sent, 'seq', 0, 0, tiled=True)  22.9 us
    all_to_all x1, blocking collectives, total_over_devices(): lax.all_to_all(whole, 'event', 0, 0, axis_index_groups=lines, tiled=True)  14.2 us
    all_to_all x1, blocking collectives, per_device(): lax.all_to_all(turned, 'seq', 0, 0, tiled=True).reshape(width, points)  11.4 us
    all_to_all x1, blocking collectives, total_over_devices(): lax.all_to_all(parts, everywhere, 0, 0, axis_index_groups=planes, tiled=T...  11.1 us
    all_to_all x1, blocking collectives, total_over_devices(): lax.all_to_all(whole, everywhere, 0, 0, axis_index_groups=planes, tiled=T...  10.6 us
    pallas_call x1, Pallas kernels, attend(): pl.pallas_call(functools.partial(attend_kernel, peers, per_peer), out_sha...  10.3 us
    pallas_call x1, Pallas kernels, contrast(): pl.pallas_call(contrast_kernel, out_shape=(half, jax.ShapeDtypeStruct((wi...  6.54 us
  transfers between devices with their start and end apart: 2, of which 2 were waited for; matrix products, arithmetic and copies ran while one was open for 0% of the time, Pallas kernels for 1%

profile of v5, /device:TPU:1, one launch (start us, length us, event | category | flops | bytes accessed | tf_op | source)
XLA Modules:
  0.0 136.4 jit_solution(7661625504584554358)
XLA Ops:
  0.6 1.9 %pack_heads.1 = bf16[8,200,384]{2,1,0:T(8,128)(2,1)S(1)} custom-call(bf16[384,512]{1,0:T(8,128)(2,1)} %bitcast.20, bf16[384,512]{1,0:T(8,128)(2,1)} %bitcast.21, bf16[384,512]{1,0:T(8,128)(2,1)} %bitcast.22, s32[3,1,24]{2,1,0:T(1,128)} %bitcast.23), custom_call_target="tpu_custom_call" | custom-call | tf_op jit(solution)/shard_map/pack_heads/pallas_call | solution.py:103
  2.5 0.0 copy-start.1
  2.5 0.0 copy-start.4
  2.6 22.9 %all_to_all.30.got_ref = bf16[8,200,384]{2,1,0:T(8,128)(2,1)S(1)} all-to-all(bf16[8,200,384]{2,1,0:T(8,128)(2,1)S(1)} %pack_heads.1), channel_id=1, replica_groups=mesh['view'=2,'seq'=8,'event'=16] {'seq'}, dimensions={0} | all-to-all | bytes 2457600 | tf_op jit(solution)/shard_map/all_to_all | solution.py:560
  25.5 10.3 %attend.1 = bf16[8,64,384]{2,1,0:T(8,128)(2,1)S(1)} custom-call(s32[24,32]{1,0:T(8,128)S(1)} %reshape.22.table_ref, bf16[8,200,384]{2,1,0:T(8,128)(2,1)S(1)} %all_to_all.30.got_ref), custom_call_target="tpu_custom_call" | custom-call | tf_op jit(solution)/shard_map/attend/pallas_call | solution.py:221
  35.7 11.4 %all_to_all.31 = bf16[8,64,384]{2,1,0:T(8,128)(2,1)S(1)} all-to-all(bf16[8,64,384]{2,1,0:T(8,128)(2,1)S(1)} %attend.1), channel_id=1, replica_groups=mesh['view'=2,'seq'=8,'event'=16] {'seq'}, dimensions={0} | all-to-all | bytes 786432 | tf_op jit(solution)/shard_map/all_to_all | solution.py:564
  47.2 2.1 %hand_out.1 = (bf16[384,512]{1,0:T(8,128)(2,1)}, bf16[16,512,128]{2,1,0:T(8,128)(2,1)S(1)}, bf16[512,256]{1,0:T(8,128)(2,1)S(1)}) custom-call(bf16[512,384]{1,0:T(8,128)(2,1)S(1)} %bitcast.13, s32[16,128]{1,0:T(8,128)S(1)} %bitcast.14, s32[1,256]{1,0:T(1,128)S(1)} %bitcast.17), custom_call_target="tpu_custom_call" | custom-call | tf_op jit(solution)/shard_map/hand_out/pallas_call | solution.py:271
  49.2 0.0 copy-start
  49.2 0.0 copy-start.2
  49.3 0.0 copy-start.3
  49.3 35.3 %all_to_all.32.cand_ref = bf16[16,512,128]{2,1,0:T(8,128)(2,1)S(1)} all-to-all(bf16[16,512,128]{2,1,0:T(8,128)(2,1)S(1)} %get-tuple-element.16), channel_id=1, replica_groups=mesh['view'=2,'seq'=8,'event'=16] {'view','seq'}, dimensions={0} | all-to-all | bytes 4194304 | tf_op jit(solution)/shard_map/all_to_all | solution.py:566
  84.6 6.5 %contrast.1 = (bf16[16,72,128]{2,1,0:T(8,128)(2,1)S(1)}, bf16[512,2048]{1,0:T(8,128)(2,1)S(1)}, bf16[512,256]{1,0:T(8,128)(2,1)S(1)}) custom-call(bf16[16,512,128]{2,1,0:T(8,128)(2,1)S(1)} %all_to_all.32.cand_ref, bf16[512,256]{1,0:T(8,128)(2,1)S(1)} %get-tuple-element.17.anchor_ref, bf16[512,512]{1,0:T(8,128)(2,1)S(1)} %copy-done, s32[1,256]{1,0:T(1,128)S(1)} %bitcast.15, ...), custom_call_target="tpu_custom_call" | custom-call | tf_op jit(solution)/shard_map/contrast/pallas_call | solution.py:424
  91.2 1.3 collective-permute-start
  92.4 0.8 keep.1.one_ref
  93.2 0.4 collective-permute-done.two_ref
  93.6 0.1 core_sum.1
  93.7 11.1 %all_to_all.33.got_ref = bf16[16,72,128]{2,1,0:T(8,128)(2,1)S(1)} all-to-all(bf16[16,72,128]{2,1,0:T(8,128)(2,1)S(1)} %core_sum.1), channel_id=1, replica_groups={{0,8,32,40,64,72,96,104,128,136,160,168,192,200,224,232},{1,9,33,41,65,..., dimensions={0} | all-to-all | bytes 589824 | tf_op jit(solution)/shard_map/all_to_all | solution.py:527
  104.8 0.1 first_sum.1
  104.8 14.2 %all_to_all.34.got_ref = bf16[8,72,128]{2,1,0:T(8,128)(2,1)S(1)} all-to-all(bf16[8,72,128]{2,1,0:T(8,128)(2,1)S(1)} %first_sum.1), channel_id=1, replica_groups={{0,1,2,3,4,5,6,7},{8,9,10,11,12,13,14,15},{16,17,18,19,20,21,22,23},{24..., dimensions={0} | all-to-all | bytes 294912 | tf_op jit(solution)/shard_map/all_to_all | solution.py:531
  119.0 0.5 last_sum.1
  119.6 10.6 %all_to_all.35 = bf16[16,32,256]{2,1,0:T(8,128)(2,1)S(1)} all-to-all(bf16[16,32,256]{2,1,0:T(8,128)(2,1)S(1)} %get-tuple-element.21), channel_id=1, replica_groups={{0,8,32,40,64,72,96,104,128,136,160,168,192,200,224,232},{1,9,33,41,65,..., dimensions={0} | all-to-all | bytes 524288 | tf_op jit(solution)/shard_map/all_to_all | solution.py:541
  130.2 3.9 %collective-permute-start.1 = (bf16[512,256]{1,0:T(8,128)(2,1)S(1)}, bf16[512,256]{1,0:T(8,128)(2,1)S(1)}, u32[]{:S(2)}, u32[]{:S(2)}) collective-permute-start(bf16[512,256]{1,0:T(8,128)(2,1)S(1)} %bitcast.18), channel_id=1, source_target_pairs={{0,16},{16,0},{32,48},{48,32},{64,80},{80,64},{96,112},{112,96},{1... | collective-permute-start | bytes 786440 | tf_op jit(solution)/shard_map/ppermute | solution.py:504
  134.1 1.2 collective-permute-done.1
  135.2 1.1 fusion
  (7 shorter events, 0.0 us)
Async XLA Ops:
  2.5 44.6 %copy-start.1 = (s32[1,1,16,128]{3,2,1,0:T(8,128)S(1)}, s32[1,1,16,128]{3,2,1,0:T(8,128)}, u32[]{:S(2)}) copy-start(s32[1,1,16,128]{3,2,1,0:T(8,128)} %param.14) | copy-start | bytes 24580
  2.5 44.6 %copy-start.4 = (s32[1,1,256]{2,1,0:T(1,128)S(1)}, s32[1,1,256]{2,1,0:T(1,128)}, u32[]{:S(2)}) copy-start(s32[1,1,256]{2,1,0:T(1,128)} %param.15) | copy-start | bytes 3076
  49.2 35.4 %copy-start = (bf16[512,512]{1,0:T(8,128)(2,1)S(1)}, bf16[512,512]{1,0:T(8,128)(2,1)}, u32[]{:S(2)}) copy-start(bf16[512,512]{1,0:T(8,128)(2,1)} %weight_ref.1) | copy-start | bytes 1572868
  49.2 35.4 %copy-start.2 = (s32[1,1,256]{2,1,0:T(1,128)S(1)}, s32[1,1,256]{2,1,0:T(1,128)}, u32[]{:S(2)}) copy-start(s32[1,1,256]{2,1,0:T(1,128)} %param.16) | copy-start | bytes 3076
  49.3 35.4 %copy-start.3 = (s32[1,1,256]{2,1,0:T(1,128)S(1)}, s32[1,1,256]{2,1,0:T(1,128)}, u32[]{:S(2)}) copy-start(s32[1,1,256]{2,1,0:T(1,128)} %param.17) | copy-start | bytes 3076
  91.2 2.5 %collective-permute-start = (bf16[16,72,128]{2,1,0:T(8,128)(2,1)S(1)}, bf16[16,72,128]{2,1,0:T(8,128)(2,1)S(1)}, u32[]{:S(2)}, u32[]{:S(2)}) collective-permute-start(bf16[16,72,128]{2,1,0:T(8,128)(2,1)S(1)} %get-tuple-element.20.away_ref), channel_id=1, source_target_pairs={{0,16},{16,0},{32,48},{48,32},{64,80},{80,64},{96,112},{112,96},{1... | collective-permute-start | bytes 884744 | tf_op jit(solution)/shard_map/ppermute | solution.py:504
  130.2 5.0 %collective-permute-start.1 = (bf16[512,256]{1,0:T(8,128)(2,1)S(1)}, bf16[512,256]{1,0:T(8,128)(2,1)S(1)}, u32[]{:S(2)}, u32[]{:S(2)}) collective-permute-start(bf16[512,256]{1,0:T(8,128)(2,1)S(1)} %bitcast.18), channel_id=1, source_target_pairs={{0,16},{16,0},{32,48},{48,32},{64,80},{80,64},{96,112},{112,96},{1... | collective-permute-start | bytes 786440 | tf_op jit(solution)/shard_map/ppermute | solution.py:504

commit v6 on v4

--- a/solution.py
+++ b/solution.py
@@ -11,7 +11,7 @@
 BLOCK = 128
 SHARPNESS_SCALE = 0.07
 GROUP = 2
-ITEMS = 6
+ITEMS = 8
 EXTRA = 8
 ONES = 16
 EVENT_RUN = 8
@@ -165,9 +165,22 @@
             jnp.where(end, 0, real),
         )
 
-    def turn(t, carry):
+    def turn(t, carry, sums=True, weights=True, scores=True):
         best, at_scores, at_weights, at_sums = carry
-        total = jnp.where(t < 3, 0.0, accum[...])
+        if sums:
+            take_sums(at_sums)
+        if weights:
+            best = take_weights(best, at_weights)
+        if not scores:
+            return best, at_scores, at_scores, at_weights
+        take_scores(at_scores)
+        following = [after(at_scores[-1])]
+        for n in range(ITEMS - 1):
+            following.append(after(following[-1]))
+        return best, tuple(following), at_scores, at_weights
+
+    def take_sums(at_sums):
+        total = accum[...]
         for n, (row, step, real) in enumerate(at_sums):
             first = step * GROUP
             count = jnp.where(real == 1, table_ref[row, blocks], 0)
@@ -184,34 +197,36 @@
                 total[head : 2 * head, BLOCK : 2 * BLOCK] * share[:, BLOCK : 2 * BLOCK]
             ).astype(BF16)
         accum[...] = total
+
+    def take_weights(best, at_weights):
         for n, (row, step, real) in enumerate(at_weights):
             best = jnp.where(jnp.logical_and(step == 0, real == 1), NEGATIVE, best)
             new_best = jnp.maximum(best, peak[n, 0:1, :])
             weighed[n] = jnp.exp2(scored[n] - new_best).astype(BF16)
             fade[n] = jnp.broadcast_to(jnp.exp2(best - new_best), (8, 2 * BLOCK))
             best = new_best
+        return best
+
+    def take_scores(at_scores):
         for n, (row, step, real) in enumerate(at_scores):
             picked = [kb[table_ref[row, step * GROUP + g]] for g in range(GROUP)]
             scores = dot(jnp.concatenate(picked, axis=0), qb[row])
             scored[n] = scores
             top = jnp.max(scores.reshape(GROUP * BLOCK // 8, 8, 2 * BLOCK), axis=0)
             peak[n] = jnp.broadcast_to(jnp.max(top, axis=0, keepdims=True), (8, 2 * BLOCK))
-        following = [after(at_scores[-1])]
-        for n in range(ITEMS - 1):
-            following.append(after(following[-1]))
-        return best, tuple(following), at_scores, at_weights
 
     zero = jnp.int32(0)
     items_at = [(zero, zero, jnp.int32(1))]
     for n in range(ITEMS - 1):
         items_at.append(after(items_at[-1]))
     idle = ((zero, zero, zero),) * ITEMS
-    lax.fori_loop(
-        0,
-        (items + ITEMS - 1) // ITEMS + 2,
-        turn,
-        (jnp.full((1, 2 * BLOCK), NEGATIVE, F32), tuple(items_at), idle, idle),
-    )
+    accum[...] = jnp.zeros_like(accum)
+    carry = (jnp.full((1, 2 * BLOCK), NEGATIVE, F32), tuple(items_at), idle, idle)
+    carry = turn(0, carry, sums=False, weights=False)
+    carry = turn(1, carry, sums=False)
+    carry = lax.fori_loop(2, (items + ITEMS - 1) // ITEMS, turn, carry)
+    carry = turn(0, carry, scores=False)
+    turn(0, carry, weights=False, scores=False)
 
 
 def attend(table, got, peers):

time: 138 us -> 136 us (0.986)
  blocking collectives: 108 us -> 106 us
    all_to_all x1, blocking collectives: 34.8 us -> 32.6 us  [per_device(): incoming = lax.all_to_all(outgoing, ('view', 'seq'), 0, 0, tiled=True)]
where the time goes in v6:
time: 136 us
  blocking collectives  106 us (78%)
  Pallas kernels  21.1 us (16%)
  starting transfers between devices  5.13 us (4%)
  waiting for transfers between devices  2.37 us (2%)
    all_to_all x1, blocking collectives, per_device(): incoming = lax.all_to_all(outgoing, ('view', 'seq'), 0, 0, tiled=True)  32.6 us
    all_to_all x1, blocking collectives, per_device(): got = lax.all_to_all(sent, 'seq', 0, 0, tiled=True)  22.9 us
    all_to_all x1, blocking collectives, total_over_devices(): lax.all_to_all(whole, 'event', 0, 0, axis_index_groups=lines, tiled=True)  17.4 us
    all_to_all x1, blocking collectives, per_device(): lax.all_to_all(turned, 'seq', 0, 0, tiled=True).reshape(width, points)  11.4 us
    all_to_all x1, blocking collectives, total_over_devices(): lax.all_to_all(parts, everywhere, 0, 0, axis_index_groups=planes, tiled=T...  11.1 us
    all_to_all x1, blocking collectives, total_over_devices(): lax.all_to_all(whole, everywhere, 0, 0, axis_index_groups=planes, tiled=T...  10.6 us
    pallas_call x1, Pallas kernels, attend(): pl.pallas_call(functools.partial(attend_kernel, peers, per_peer), out_sha...  10.2 us
    pallas_call x1, Pallas kernels, contrast(): pl.pallas_call(contrast_kernel, out_shape=(half,) * 2, in_specs=[pl.Block...  6.24 us
  transfers between devices with their start and end apart: 2, of which 2 were waited for; matrix products, arithmetic and copies ran while one was open for 0% of the time, Pallas kernels for 0%

profile of v6, /device:TPU:1, one launch (start us, length us, event | category | flops | bytes accessed | tf_op | source)
XLA Modules:
  0.0 136.4 jit_solution(14393472439152311635)
XLA Ops:
  0.6 1.9 %pack_heads.1 = bf16[8,200,384]{2,1,0:T(8,128)(2,1)S(1)} custom-call(bf16[384,512]{1,0:T(8,128)(2,1)} %bitcast.20, bf16[384,512]{1,0:T(8,128)(2,1)} %bitcast.21, bf16[384,512]{1,0:T(8,128)(2,1)} %bitcast.22, s32[3,1,24]{2,1,0:T(1,128)} %bitcast.23), custom_call_target="tpu_custom_call" | custom-call | tf_op jit(solution)/shard_map/pack_heads/pallas_call | solution.py:103
  2.5 22.9 %all_to_all.30.got_ref = bf16[8,200,384]{2,1,0:T(8,128)(2,1)S(1)} all-to-all(bf16[8,200,384]{2,1,0:T(8,128)(2,1)S(1)} %pack_heads.1), channel_id=1, replica_groups=mesh['view'=2,'seq'=8,'event'=16] {'seq'}, dimensions={0} | all-to-all | bytes 2457600 | tf_op jit(solution)/shard_map/all_to_all | solution.py:537
  25.4 0.0 copy-start.4
  25.5 10.2 %attend.1 = bf16[8,64,384]{2,1,0:T(8,128)(2,1)S(1)} custom-call(s32[24,32]{1,0:T(8,128)S(1)} %reshape.22.table_ref, bf16[8,200,384]{2,1,0:T(8,128)(2,1)S(1)} %all_to_all.30.got_ref), custom_call_target="tpu_custom_call" | custom-call | tf_op jit(solution)/shard_map/attend/pallas_call | solution.py:236
  35.7 11.4 %all_to_all.31 = bf16[8,64,384]{2,1,0:T(8,128)(2,1)S(1)} all-to-all(bf16[8,64,384]{2,1,0:T(8,128)(2,1)S(1)} %attend.1), channel_id=1, replica_groups=mesh['view'=2,'seq'=8,'event'=16] {'seq'}, dimensions={0} | all-to-all | bytes 786432 | tf_op jit(solution)/shard_map/all_to_all | solution.py:541
  47.1 0.0 copy-done.1
  47.1 0.0 copy-done.4
  47.1 2.1 %hand_out.1 = (bf16[384,512]{1,0:T(8,128)(2,1)}, bf16[16,512,128]{2,1,0:T(8,128)(2,1)S(1)}, bf16[512,256]{1,0:T(8,128)(2,1)S(1)}) custom-call(bf16[512,384]{1,0:T(8,128)(2,1)S(1)} %bitcast.13, s32[16,128]{1,0:T(8,128)S(1)} %bitcast.14, s32[1,256]{1,0:T(1,128)S(1)} %bitcast.17), custom_call_target="tpu_custom_call" | custom-call | tf_op jit(solution)/shard_map/hand_out/pallas_call | solution.py:281
  49.2 32.6 %all_to_all.32.cand_ref = bf16[16,512,128]{2,1,0:T(8,128)(2,1)S(1)} all-to-all(bf16[16,512,128]{2,1,0:T(8,128)(2,1)S(1)} %get-tuple-element.15), channel_id=1, replica_groups=mesh['view'=2,'seq'=8,'event'=16] {'view','seq'}, dimensions={0} | all-to-all | bytes 4194304 | tf_op jit(solution)/shard_map/all_to_all | solution.py:543
  81.8 0.0 copy-done
  81.8 0.0 copy-done.2
  81.8 0.0 copy-done.3
  81.8 6.2 %contrast.1 = (bf16[16,72,128]{2,1,0:T(8,128)(2,1)S(1)}, bf16[16,72,128]{2,1,0:T(8,128)(2,1)S(1)}) custom-call(bf16[16,512,128]{2,1,0:T(8,128)(2,1)S(1)} %all_to_all.32.cand_ref, bf16[512,256]{1,0:T(8,128)(2,1)S(1)} %get-tuple-element.16.anchor_ref, bf16[512,512]{1,0:T(8,128)(2,1)S(1)} %copy-done, s32[1,256]{1,0:T(1,128)S(1)} %bitcast.15, s32[1,256]{1,0:T(1,128)S(1)} %bitcast.16), custom_call_target="tpu_custom_call" | custom-call | tf_op jit(solution)/shard_map/contrast/pallas_call | solution.py:403
  88.0 1.3 collective-permute-start
  89.3 1.2 collective-permute-done.two_ref
  90.5 0.1 core_sum.1
  90.5 11.1 %all_to_all.33.got_ref = bf16[16,72,128]{2,1,0:T(8,128)(2,1)S(1)} all-to-all(bf16[16,72,128]{2,1,0:T(8,128)(2,1)S(1)} %core_sum.1), channel_id=1, replica_groups={{0,8,32,40,64,72,96,104,128,136,160,168,192,200,224,232},{1,9,33,41,65,..., dimensions={0} | all-to-all | bytes 589824 | tf_op jit(solution)/shard_map/all_to_all | solution.py:504
  101.6 0.1 first_sum.1
  101.7 17.4 %all_to_all.34.got_ref = bf16[8,72,128]{2,1,0:T(8,128)(2,1)S(1)} all-to-all(bf16[8,72,128]{2,1,0:T(8,128)(2,1)S(1)} %first_sum.1), channel_id=1, replica_groups={{0,1,2,3,4,5,6,7},{8,9,10,11,12,13,14,15},{16,17,18,19,20,21,22,23},{24..., dimensions={0} | all-to-all | bytes 294912 | tf_op jit(solution)/shard_map/all_to_all | solution.py:508
  119.0 0.5 last_sum.1
  119.6 10.6 %all_to_all.35 = bf16[16,32,256]{2,1,0:T(8,128)(2,1)S(1)} all-to-all(bf16[16,32,256]{2,1,0:T(8,128)(2,1)S(1)} %get-tuple-element.19), channel_id=1, replica_groups={{0,8,32,40,64,72,96,104,128,136,160,168,192,200,224,232},{1,9,33,41,65,..., dimensions={0} | all-to-all | bytes 524288 | tf_op jit(solution)/shard_map/all_to_all | solution.py:518
  130.2 3.9 %collective-permute-start.1 = (bf16[512,256]{1,0:T(8,128)(2,1)S(1)}, bf16[512,256]{1,0:T(8,128)(2,1)S(1)}, u32[]{:S(2)}, u32[]{:S(2)}) collective-permute-start(bf16[512,256]{1,0:T(8,128)(2,1)S(1)} %bitcast.18), channel_id=1, source_target_pairs={{0,16},{16,0},{32,48},{48,32},{64,80},{80,64},{96,112},{112,96},{1... | collective-permute-start | bytes 786440 | tf_op jit(solution)/shard_map/ppermute | solution.py:481
  134.1 1.2 collective-permute-done.1
  135.2 1.1 fusion
  (6 shorter events, 0.0 us)
Async XLA Ops:
  25.4 21.7 %copy-start.1 = (s32[1,1,16,128]{3,2,1,0:T(8,128)S(1)}, s32[1,1,16,128]{3,2,1,0:T(8,128)}, u32[]{:S(2)}) copy-start(s32[1,1,16,128]{3,2,1,0:T(8,128)} %param.14) | copy-start | bytes 24580
  25.4 21.7 %copy-start.4 = (s32[1,1,256]{2,1,0:T(1,128)S(1)}, s32[1,1,256]{2,1,0:T(1,128)}, u32[]{:S(2)}) copy-start(s32[1,1,256]{2,1,0:T(1,128)} %param.15) | copy-start | bytes 3076
  49.2 32.6 %copy-start = (bf16[512,512]{1,0:T(8,128)(2,1)S(1)}, bf16[512,512]{1,0:T(8,128)(2,1)}, u32[]{:S(2)}) copy-start(bf16[512,512]{1,0:T(8,128)(2,1)} %weight_ref.1) | copy-start | bytes 1572868
  49.2 32.6 %copy-start.2 = (s32[1,1,256]{2,1,0:T(1,128)S(1)}, s32[1,1,256]{2,1,0:T(1,128)}, u32[]{:S(2)}) copy-start(s32[1,1,256]{2,1,0:T(1,128)} %param.16) | copy-start | bytes 3076
  49.2 32.6 %copy-start.3 = (s32[1,1,256]{2,1,0:T(1,128)S(1)}, s32[1,1,256]{2,1,0:T(1,128)}, u32[]{:S(2)}) copy-start(s32[1,1,256]{2,1,0:T(1,128)} %param.17) | copy-start | bytes 3076
  88.0 2.5 %collective-permute-start = (bf16[16,72,128]{2,1,0:T(8,128)(2,1)S(1)}, bf16[16,72,128]{2,1,0:T(8,128)(2,1)S(1)}, u32[]{:S(2)}, u32[]{:S(2)}) collective-permute-start(bf16[16,72,128]{2,1,0:T(8,128)(2,1)S(1)} %get-tuple-element.18), channel_id=1, source_target_pairs={{0,16},{16,0},{32,48},{48,32},{64,80},{80,64},{96,112},{112,96},{1... | collective-permute-start | bytes 884744 | tf_op jit(solution)/shard_map/ppermute | solution.py:481
  130.2 5.0 %collective-permute-start.1 = (bf16[512,256]{1,0:T(8,128)(2,1)S(1)}, bf16[512,256]{1,0:T(8,128)(2,1)S(1)}, u32[]{:S(2)}, u32[]{:S(2)}) collective-permute-start(bf16[512,256]{1,0:T(8,128)(2,1)S(1)} %bitcast.18), channel_id=1, source_target_pairs={{0,16},{16,0},{32,48},{48,32},{64,80},{80,64},{96,112},{112,96},{1... | collective-permute-start | bytes 786440 | tf_op jit(solution)/shard_map/ppermute | solution.py:481

commit v7 on v6

--- a/solution.py
+++ b/solution.py
@@ -439,14 +439,23 @@
 
 def last_sum_kernel(got_ref, out_ref, loss_ref):
     part, loss, count = summed(got_ref)
-    rows = out_ref.shape[1]
+    rows = out_ref.shape[0]
     part = part.astype(BF16)
-    whole = jnp.concatenate(
+    out_ref[...] = jnp.concatenate(
         [part[at : at + rows, :] for at in range(0, part.shape[0], rows)], axis=1
     )
+    loss_ref[...] = loss / count
+
+
+def join_kernel(mine_ref, other_ref, out_ref):
+    core = lax.rem(lax.axis_index("seq"), 2)
+    half = mine_ref.shape[1]
+    mine, other = mine_ref[...], other_ref[...]
+    first = jnp.where(core == 0, mine, other)
+    second = jnp.where(core == 0, other, mine)
     for n in range(out_ref.shape[0]):
-        out_ref[n] = whole
-    loss_ref[...] = loss / count
+        out_ref[n, :, :half] = first
+        out_ref[n, :, half:] = second
 
 
 def core_sum_kernel(one_ref, two_ref, out_ref):
@@ -493,7 +502,7 @@
     )(*operands)
 
 
-def total_over_devices(away, kept, core, width):
+def total_over_devices(away, kept, width):
     planes, lines = groups()
     everywhere = ("view", "seq", "event")
     ways, half = len(planes[0]), width // 2
@@ -506,23 +515,24 @@
         first_sum_kernel, "first_sum", jax.ShapeDtypeStruct((len(lines[0]),) + shape[1:], BF16), got
     )
     got = lax.all_to_all(whole, "event", 0, 0, axis_index_groups=lines, tiled=True)
-    whole, loss = small(
+    mine, loss = small(
         last_sum_kernel,
         "last_sum",
         (
-            jax.ShapeDtypeStruct((ways, width // ways, half), BF16),
+            jax.ShapeDtypeStruct((width // ways, half), BF16),
             jax.ShapeDtypeStruct((1, 128), F32),
         ),
         got,
     )
-    mine = lax.all_to_all(whole, everywhere, 0, 0, axis_index_groups=planes, tiled=True)
-    mine = mine.reshape(width, half)
-    other = to_other_core(mine)
-    grad = jnp.where(
-        core == 0,
-        jnp.concatenate([mine, other], axis=1),
-        jnp.concatenate([other, mine], axis=1),
-    )
+    whole = small(
+        join_kernel,
+        "join",
+        jax.ShapeDtypeStruct((ways, width // ways, width), BF16),
+        mine,
+        to_other_core(mine),
+    )
+    grad = lax.all_to_all(whole, everywhere, 0, 0, axis_index_groups=planes, tiled=True)
+    grad = grad.reshape(width, width)
     return grad.astype(F32), loss[0, 0]
 
 
@@ -533,7 +543,6 @@
     peers = lax.axis_size("seq")
     rows = pattern.shape[2]
     sent = pack(query[0, 0], key[0, 0], value[0, 0], pattern[0, 0][:, None, :], peers)
-    sent, core = lax.optimization_barrier((sent, lax.rem(lax.axis_index("seq"), 2)))
     got = lax.all_to_all(sent, "seq", 0, 0, tiled=True)
     part = 3 * (width // peers)
     table = got[:, part : part + rows, :LIST].astype(jnp.int32).reshape(peers * rows, LIST)
@@ -545,7 +554,7 @@
     away, kept = contrast(
         incoming, anchors, out_weight, positive_slot[0], anchor_live[0], ways
     )
-    grad_total, loss = total_over_devices(away, kept, core, width)
+    grad_total, loss = total_over_devices(away, kept, width)
     return (mixed[None, None], grad_total, loss)
 
 

time: 136 us -> 138 us (1.015)
  blocking collectives: 106 us -> 109 us
    all_to_all x1, blocking collectives: 10.6 us -> 13.4 us  [total_over_devices(): lax.all_to_all(whole, everywhere, 0, 0, axis_index_groups=planes, tiled=T...]
where the time goes in v7:
time: 138 us
  blocking collectives  109 us (79%)
  Pallas kernels  21.1 us (15%)
  starting transfers between devices  4.16 us (3%)
  waiting for transfers between devices  2.05 us (1%)
    all_to_all x1, blocking collectives, per_device(): incoming = lax.all_to_all(outgoing, ('view', 'seq'), 0, 0, tiled=True)  33.2 us
    all_to_all x1, blocking collectives, per_device(): got = lax.all_to_all(sent, 'seq', 0, 0, tiled=True)  22.9 us
    all_to_all x1, blocking collectives, total_over_devices(): lax.all_to_all(whole, 'event', 0, 0, axis_index_groups=lines, tiled=True)  16.9 us
    all_to_all x1, blocking collectives, total_over_devices(): lax.all_to_all(whole, everywhere, 0, 0, axis_index_groups=planes, tiled=T...  13.4 us
    all_to_all x1, blocking collectives, per_device(): lax.all_to_all(turned, 'seq', 0, 0, tiled=True).reshape(width, points)  11.4 us
    all_to_all x1, blocking collectives, total_over_devices(): lax.all_to_all(parts, everywhere, 0, 0, axis_index_groups=planes, tiled=T...  11.1 us
    pallas_call x1, Pallas kernels, attend(): pl.pallas_call(functools.partial(attend_kernel, peers, per_peer), out_sha...  10.2 us
    pallas_call x1, Pallas kernels, contrast(): pl.pallas_call(contrast_kernel, out_shape=(half,) * 2, in_specs=[pl.Block...  6.23 us
  transfers between devices with their start and end apart: 2, of which 2 were waited for; matrix products, arithmetic and copies ran while one was open for 0% of the time, Pallas kernels for 0%

profile of v7, /device:TPU:1, one launch (start us, length us, event | category | flops | bytes accessed | tf_op | source)
XLA Modules:
  0.0 138.1 jit_solution(14518696393373577080)
XLA Ops:
  0.6 1.9 %pack_heads.1 = bf16[8,200,384]{2,1,0:T(8,128)(2,1)S(1)} custom-call(bf16[384,512]{1,0:T(8,128)(2,1)} %bitcast.20, bf16[384,512]{1,0:T(8,128)(2,1)} %bitcast.21, bf16[384,512]{1,0:T(8,128)(2,1)} %bitcast.22, s32[3,1,24]{2,1,0:T(1,128)} %bitcast.23), custom_call_target="tpu_custom_call" | custom-call | tf_op jit(solution)/shard_map/pack_heads/pallas_call | solution.py:103
  2.5 22.9 %all_to_all.30.got_ref = bf16[8,200,384]{2,1,0:T(8,128)(2,1)S(1)} all-to-all(bf16[8,200,384]{2,1,0:T(8,128)(2,1)S(1)} %pack_heads.1), channel_id=1, replica_groups=mesh['view'=2,'seq'=8,'event'=16] {'seq'}, dimensions={0} | all-to-all | bytes 2457600 | tf_op jit(solution)/shard_map/all_to_all | solution.py:546
  25.4 0.0 copy-start.4
  25.5 10.2 %attend.1 = bf16[8,64,384]{2,1,0:T(8,128)(2,1)S(1)} custom-call(s32[24,32]{1,0:T(8,128)S(1)} %reshape.21.table_ref, bf16[8,200,384]{2,1,0:T(8,128)(2,1)S(1)} %all_to_all.30.got_ref), custom_call_target="tpu_custom_call" | custom-call | tf_op jit(solution)/shard_map/attend/pallas_call | solution.py:236
  35.7 11.4 %all_to_all.31 = bf16[8,64,384]{2,1,0:T(8,128)(2,1)S(1)} all-to-all(bf16[8,64,384]{2,1,0:T(8,128)(2,1)S(1)} %attend.1), channel_id=1, replica_groups=mesh['view'=2,'seq'=8,'event'=16] {'seq'}, dimensions={0} | all-to-all | bytes 786432 | tf_op jit(solution)/shard_map/all_to_all | solution.py:550
  47.1 0.0 copy-done.1
  47.1 0.0 copy-done.4
  47.1 2.1 %hand_out.1 = (bf16[384,512]{1,0:T(8,128)(2,1)}, bf16[16,512,128]{2,1,0:T(8,128)(2,1)S(1)}, bf16[512,256]{1,0:T(8,128)(2,1)S(1)}) custom-call(bf16[512,384]{1,0:T(8,128)(2,1)S(1)} %bitcast.15, s32[16,128]{1,0:T(8,128)S(1)} %bitcast.16, s32[1,256]{1,0:T(1,128)S(1)} %bitcast.19), custom_call_target="tpu_custom_call" | custom-call | tf_op jit(solution)/shard_map/hand_out/pallas_call | solution.py:281
  49.2 33.2 %all_to_all.32.cand_ref = bf16[16,512,128]{2,1,0:T(8,128)(2,1)S(1)} all-to-all(bf16[16,512,128]{2,1,0:T(8,128)(2,1)S(1)} %get-tuple-element.11), channel_id=1, replica_groups=mesh['view'=2,'seq'=8,'event'=16] {'view','seq'}, dimensions={0} | all-to-all | bytes 4194304 | tf_op jit(solution)/shard_map/all_to_all | solution.py:552
  82.4 0.0 copy-done
  82.4 0.0 copy-done.2
  82.4 0.0 copy-done.3
  82.4 6.2 %contrast.1 = (bf16[16,72,128]{2,1,0:T(8,128)(2,1)S(1)}, bf16[16,72,128]{2,1,0:T(8,128)(2,1)S(1)}) custom-call(bf16[16,512,128]{2,1,0:T(8,128)(2,1)S(1)} %all_to_all.32.cand_ref, bf16[512,256]{1,0:T(8,128)(2,1)S(1)} %get-tuple-element.12.anchor_ref, bf16[512,512]{1,0:T(8,128)(2,1)S(1)} %copy-done, s32[1,256]{1,0:T(1,128)S(1)} %bitcast.17, s32[1,256]{1,0:T(1,128)S(1)} %bitcast.18), custom_call_target="tpu_custom_call" | custom-call | tf_op jit(solution)/shard_map/contrast/pallas_call | solution.py:403
  88.6 1.3 collective-permute-start
  89.9 1.2 collective-permute-done.two_ref
  91.1 0.1 core_sum.1
  91.2 11.1 %all_to_all.33.got_ref = bf16[16,72,128]{2,1,0:T(8,128)(2,1)S(1)} all-to-all(bf16[16,72,128]{2,1,0:T(8,128)(2,1)S(1)} %core_sum.1), channel_id=1, replica_groups={{0,8,32,40,64,72,96,104,128,136,160,168,192,200,224,232},{1,9,33,41,65,..., dimensions={0} | all-to-all | bytes 589824 | tf_op jit(solution)/shard_map/all_to_all | solution.py:513
  102.2 0.1 first_sum.1
  102.3 16.9 %all_to_all.34.got_ref = bf16[8,72,128]{2,1,0:T(8,128)(2,1)S(1)} all-to-all(bf16[8,72,128]{2,1,0:T(8,128)(2,1)S(1)} %first_sum.1), channel_id=1, replica_groups={{0,1,2,3,4,5,6,7},{8,9,10,11,12,13,14,15},{16,17,18,19,20,21,22,23},{24..., dimensions={0} | all-to-all | bytes 294912 | tf_op jit(solution)/shard_map/all_to_all | solution.py:517
  119.2 0.5 last_sum.1
  119.8 2.9 %collective-permute-start.1 = (bf16[32,256]{1,0:T(8,128)(2,1)S(1)}, bf16[32,256]{1,0:T(8,128)(2,1)S(1)}, u32[]{:S(2)}, u32[]{:S(2)}) collective-permute-start(bf16[32,256]{1,0:T(8,128)(2,1)S(1)} %get-tuple-element.15.mine_ref), channel_id=1, source_target_pairs={{0,16},{16,0},{32,48},{48,32},{64,80},{80,64},{96,112},{112,96},{1... | collective-permute-start | bytes 49160 | tf_op jit(solution)/shard_map/ppermute | solution.py:490
  122.7 0.8 collective-permute-done.1.other_ref
  123.6 13.4 %all_to_all.35 = bf16[16,32,512]{2,1,0:T(8,128)(2,1)S(1)} all-to-all(bf16[16,32,512]{2,1,0:T(8,128)(2,1)S(1)} %join.1), channel_id=1, replica_groups={{0,8,32,40,64,72,96,104,128,136,160,168,192,200,224,232},{1,9,33,41,65,..., dimensions={0} | all-to-all | bytes 1048576 | tf_op jit(solution)/shard_map/all_to_all | solution.py:534
  136.9 1.1 bitcast_convert_fusion
  (7 shorter events, 0.1 us)
Async XLA Ops:
  25.4 21.7 %copy-start.1 = (s32[1,1,16,128]{3,2,1,0:T(8,128)S(1)}, s32[1,1,16,128]{3,2,1,0:T(8,128)}, u32[]{:S(2)}) copy-start(s32[1,1,16,128]{3,2,1,0:T(8,128)} %param.14) | copy-start | bytes 24580
  25.4 21.7 %copy-start.4 = (s32[1,1,256]{2,1,0:T(1,128)S(1)}, s32[1,1,256]{2,1,0:T(1,128)}, u32[]{:S(2)}) copy-start(s32[1,1,256]{2,1,0:T(1,128)} %param.15) | copy-start | bytes 3076
  49.2 33.2 %copy-start = (bf16[512,512]{1,0:T(8,128)(2,1)S(1)}, bf16[512,512]{1,0:T(8,128)(2,1)}, u32[]{:S(2)}) copy-start(bf16[512,512]{1,0:T(8,128)(2,1)} %weight_ref.1) | copy-start | bytes 1572868
  49.2 33.2 %copy-start.2 = (s32[1,1,256]{2,1,0:T(1,128)S(1)}, s32[1,1,256]{2,1,0:T(1,128)}, u32[]{:S(2)}) copy-start(s32[1,1,256]{2,1,0:T(1,128)} %param.16) | copy-start | bytes 3076
  49.2 33.2 %copy-start.3 = (s32[1,1,256]{2,1,0:T(1,128)S(1)}, s32[1,1,256]{2,1,0:T(1,128)}, u32[]{:S(2)}) copy-start(s32[1,1,256]{2,1,0:T(1,128)} %param.17) | copy-start | bytes 3076
  88.6 2.5 %collective-permute-start = (bf16[16,72,128]{2,1,0:T(8,128)(2,1)S(1)}, bf16[16,72,128]{2,1,0:T(8,128)(2,1)S(1)}, u32[]{:S(2)}, u32[]{:S(2)}) collective-permute-start(bf16[16,72,128]{2,1,0:T(8,128)(2,1)S(1)} %get-tuple-element.14), channel_id=1, source_target_pairs={{0,16},{16,0},{32,48},{48,32},{64,80},{80,64},{96,112},{112,96},{1... | collective-permute-start | bytes 884744 | tf_op jit(solution)/shard_map/ppermute | solution.py:490
  119.8 3.7 %collective-permute-start.1 = (bf16[32,256]{1,0:T(8,128)(2,1)S(1)}, bf16[32,256]{1,0:T(8,128)(2,1)S(1)}, u32[]{:S(2)}, u32[]{:S(2)}) collective-permute-start(bf16[32,256]{1,0:T(8,128)(2,1)S(1)} %get-tuple-element.15.mine_ref), channel_id=1, source_target_pairs={{0,16},{16,0},{32,48},{48,32},{64,80},{80,64},{96,112},{112,96},{1... | collective-permute-start | bytes 49160 | tf_op jit(solution)/shard_map/ppermute | solution.py:490
